TPU v7x, 32 devices: a whole 2x2x4 slice. The times are simulated.
32 devices in a mesh: replica: 4 (over y, core), shard: 8 (over z, x).
Axes of the slice: x: 2, y: 2, z: 4, core: 2. Of those that a mesh axis runs over, the one named last changes fastest.
Arguments:
- tokens: bfloat16 [32768, 768], P(('replica', 'shard')), may hold values from -6 to 6
- cotangent: bfloat16 [32768, 768], P(('replica', 'shard')), may hold values from -6 to 6
- seq_units: int32 [4, 16], P('replica'), may hold values from 16 to 112, as said below
- seq_order: int32 [4, 16], P('replica'), may hold values from 0 to 15, as said below
- share_start: int32 [4, 16], P('replica'), may hold values from 0 to 1023, as said below
- stacked_weight: bfloat16 [768, 2304], P('shard'), may hold values from -0.21875 to 0.21875
- query_bias: bfloat16 [768], P('shard'), may hold values from -3 to 3
- value_bias: bfloat16 [768], P('shard'), may hold values from -0.119628906 to 0.119628906
- out_weight: bfloat16 [768, 768], P('shard'), may hold values from -3.5 to 3.5
- out_bias: bfloat16 [768], P('shard'), may hold values from -1.1953125 to 1.1953125
- first_gain: bfloat16 [768], P('shard'), may hold values from 0.25 to 1.75
- first_shift: bfloat16 [768], P('shard'), may hold values from -1.796875 to 1.796875
- up_weight: bfloat16 [768, 3072], P('shard'), may hold values from -0.21875 to 0.21875
- up_bias: bfloat16 [3072], P('shard'), may hold values from -1.796875 to 1.796875
- down_weight: bfloat16 [3072, 768], P('shard'), may hold values from -0.15625 to 0.15625
- down_bias: bfloat16 [768], P('shard'), may hold values from -1.1953125 to 1.1953125
- second_gain: bfloat16 [768], P('shard'), may hold values from 0.25 to 1.75
- second_shift: bfloat16 [768], P('shard'), may hold values from -1.796875 to 1.796875
Outputs:
- layer_out: bfloat16 [32768, 768], P(('replica', 'shard'))
- input_grad: bfloat16 [32768, 768], P(('replica', 'shard'))
- stacked_grad: float32 [768, 2304], P('shard')
- query_bias_grad: float32 [768], P('shard')
- value_bias_grad: float32 [768], P('shard')
- out_weight_grad: float32 [768, 768], P('shard')
- out_bias_grad: float32 [768], P('shard')
- first_gain_grad: float32 [768], P('shard')
- first_shift_grad: float32 [768], P('shard')
- up_weight_grad: float32 [768, 3072], P('shard')
- up_bias_grad: float32 [3072], P('shard')
- down_weight_grad: float32 [3072, 768], P('shard')
- down_bias_grad: float32 [768], P('shard')
- second_gain_grad: float32 [768], P('shard')
- second_shift_grad: float32 [768], P('shard')
Inputs may be any that keep to these rules, and one draw needn't show every extreme that they name: `seq_units`: lengths in units of 8 tokens. After the deal each device of a group owns exactly two sequences of at most 128 units together; one device owns exactly 128 units, a sequence of 112 units and one of 16. `seq_order`: each replica's row is a permutation of its 16 sequences. `share_start`: shares lie in sequence order without intersection, and the last sequence's share ends at row 1024.
All inputs are finite; a program needn't handle non-finite values.
Results may differ from a plain program's by a relative error of at most 0.02.
Values may be sent and summed in bfloat16 or wider, within the bound.
No kernel may reach another device: no remote copies, remote signals or barrier semaphores. Data moves between devices by JAX's collectives and lax.ppermute only.
A program may use at most 192 MiB of HBM per device.

v0:
```python
import math

import jax
import jax.numpy as jnp
from jax import lax
from jax.sharding import PartitionSpec as P

HEADS = 12
HEAD_DIM = 64


EPSILON = 1e-12
MASKED = -1000000000.0


def layer_norm(values, norm_gain, norm_shift):
    center = values - jnp.mean(values, -1, keepdims=True)
    spread = jnp.mean(center * center, -1, keepdims=True)
    return center * lax.rsqrt(spread + EPSILON) * norm_gain + norm_shift


def gelu_exact(values):
    return jax.nn.gelu(values, approximate=False)


def routing(lengths, deal_order, starts, row_count, dest_count):
    total_seqs = lengths.shape[0]
    per_dest = row_count // dest_count
    labels = jnp.arange(total_seqs, dtype=jnp.int32)
    chosen = (deal_order[:, None] == labels[None, :]).astype(jnp.int32)
    dealt_len = jnp.sum(chosen * lengths[None, :], 1).reshape(dest_count, 2)
    dealt_start = jnp.sum(chosen * starts[None, :], 1).reshape(dest_count, 2)
    first_len = dealt_len[:, 0:1]
    second_len = dealt_len[:, 1:2]
    position = jnp.arange(per_dest, dtype=jnp.int32)[None, :]
    in_first = position < first_len
    in_second = jnp.logical_and(position >= first_len, position < first_len + second_len)
    source_rows = jnp.where(
        in_first,
        dealt_start[:, 0:1] + position,
        jnp.where(in_second, dealt_start[:, 1:2] + position - first_len, row_count),
    )
    segments = jnp.where(in_first, 0, jnp.where(in_second, 1, 2)).astype(jnp.int32)
    placed = jnp.sum(chosen * labels[:, None], 0)
    earlier = jnp.concatenate([jnp.zeros((dest_count, 1), jnp.int32), first_len], 1).reshape(-1)
    offset = placed // 2 * per_dest + jnp.sum(chosen * earlier[:, None], 0)
    row_index = jnp.arange(row_count, dtype=jnp.int32)[:, None]
    member = jnp.logical_and(row_index >= starts[None, :], row_index < (starts + lengths)[None, :])
    landing = jnp.sum(jnp.where(member, offset[None, :] + row_index - starts[None, :], 0), 1)
    landing = landing + jnp.where(jnp.any(member, 1), 0, dest_count * per_dest)
    return (source_rows, segments, landing)


def masked_scores(query_blk, key_one, seg_query, seg_keys, score_scale):
    scores = (
        jnp.einsum("qhd,khd->hqk", query_blk, key_one, preferred_element_type=jnp.float32)
        * score_scale
    )
    return jnp.where((seg_query[:, None] == seg_keys[None, :])[None], scores, MASKED)


def shards(
    tokens,
    cotangent,
    seq_units,
    seq_order,
    share_start,
    stacked_weight,
    query_bias,
    value_bias,
    out_weight,
    out_bias,
    first_gain,
    first_shift,
    up_weight,
    up_bias,
    down_weight,
    down_bias,
    second_gain,
    second_shift,
):
    row_count, feature_count = tokens.shape
    dest_count = lax.axis_size("shard")
    per_dest = row_count // dest_count
    source_rows, segments, landing = routing(
        seq_units[0], seq_order[0], share_start[0], row_count, dest_count
    )
    zero_row = jnp.zeros((1, feature_count), jnp.bfloat16)
    flat_rows = source_rows.reshape(-1)
    token_send = jnp.take(jnp.concatenate([tokens, zero_row], 0), flat_rows, axis=0)
    grad_send = jnp.take(jnp.concatenate([cotangent, zero_row], 0), flat_rows, axis=0)
    token_recv, grad_recv = (
        lax.all_to_all(
            token_send.reshape(dest_count, per_dest, feature_count),
            "shard",
            split_axis=0,
            concat_axis=0,
            tiled=True,
        ),
        lax.all_to_all(
            grad_send.reshape(dest_count, per_dest, feature_count),
            "shard",
            split_axis=0,
            concat_axis=0,
            tiled=True,
        ),
    )
    hidden = token_recv.reshape(row_count, feature_count)
    upstream = grad_recv.reshape(row_count, feature_count).astype(jnp.float32)
    my_index = lax.axis_index("shard")
    my_segments = lax.dynamic_index_in_dim(segments, my_index, 0, keepdims=False)
    seg_rows = jnp.tile(my_segments, dest_count)
    whole_weights = (
        lax.all_gather(stacked_weight, "shard", axis=0, tiled=True),
        lax.all_gather(out_weight, "shard", axis=0, tiled=True),
        lax.all_gather(up_weight, "shard", axis=0, tiled=True),
        lax.all_gather(down_weight, "shard", axis=0, tiled=True),
        lax.all_gather(query_bias, "shard", axis=0, tiled=True),
        lax.all_gather(value_bias, "shard", axis=0, tiled=True),
        lax.all_gather(out_bias, "shard", axis=0, tiled=True),
        lax.all_gather(first_gain, "shard", axis=0, tiled=True),
        lax.all_gather(first_shift, "shard", axis=0, tiled=True),
        lax.all_gather(up_bias, "shard", axis=0, tiled=True),
        lax.all_gather(down_bias, "shard", axis=0, tiled=True),
        lax.all_gather(second_gain, "shard", axis=0, tiled=True),
        lax.all_gather(second_shift, "shard", axis=0, tiled=True),
    )
    stack_full, out_full, up_full, down_full = (
        whole_weights[0],
        whole_weights[1],
        whole_weights[2],
        whole_weights[3],
    )
    query_add = whole_weights[4].astype(jnp.float32)
    value_add = whole_weights[5].astype(jnp.float32)
    out_add = whole_weights[6].astype(jnp.float32)
    gain_first = whole_weights[7].astype(jnp.float32)
    shift_first = whole_weights[8].astype(jnp.float32)
    up_add = whole_weights[9].astype(jnp.float32)
    down_add = whole_weights[10].astype(jnp.float32)
    gain_second = whole_weights[11].astype(jnp.float32)
    shift_second = whole_weights[12].astype(jnp.float32)
    group_heads = math.gcd(HEADS, 4)
    head_groups = HEADS // group_heads
    blocks = max(1, row_count // 512)
    block_rows = row_count // blocks
    score_scale = 1.0 / math.sqrt(HEAD_DIM)
    seg_blocks = seg_rows.reshape(blocks, block_rows)

    def by_block(matrix):
        return matrix.reshape(blocks, block_rows, head_groups, group_heads, HEAD_DIM).transpose(
            2, 0, 1, 3, 4
        )

    def by_head(matrix):
        return matrix.reshape(row_count, head_groups, group_heads, HEAD_DIM).transpose(1, 0, 2, 3)

    def from_block(tensor):
        return tensor.transpose(1, 2, 0, 3, 4).reshape(row_count, feature_count)

    def from_head(tensor):
        return tensor.transpose(1, 0, 2, 3).reshape(row_count, feature_count)

    zero_add = jnp.zeros((feature_count,), jnp.float32)
    projected = (
        jnp.dot(hidden, stack_full, preferred_element_type=jnp.float32)
        + jnp.concatenate([query_add, zero_add, value_add])
    ).astype(jnp.bfloat16)
    query_grp = by_block(projected[:, :feature_count])
    key_grp = by_head(projected[:, feature_count : 2 * feature_count])
    value_grp = by_head(projected[:, 2 * feature_count :])

    def forward_group(group_items):
        query_one, key_one, value_one = group_items

        def forward_per_block(block_items):
            query_blk, seg_query = block_items
            scores = masked_scores(query_blk, key_one, seg_query, seg_rows, score_scale)
            row_peak = jnp.max(scores, -1, keepdims=True)
            log_total = row_peak + jnp.log(jnp.sum(jnp.exp(scores - row_peak), -1, keepdims=True))
            prob_low = jnp.exp(scores - log_total).astype(jnp.bfloat16)
            mixture = jnp.einsum(
                "hqk,khd->qhd", prob_low, value_one, preferred_element_type=jnp.float32
            )
            return (mixture.astype(jnp.bfloat16), log_total)

        return lax.map(forward_per_block, (query_one, seg_blocks))

    mixture, log_totals = lax.map(forward_group, (query_grp, key_grp, value_grp))
    attended = from_block(mixture)
    branch = jnp.dot(attended, out_full, preferred_element_type=jnp.float32) + out_add
    normed_first, first_pull = jax.vjp(
        layer_norm, hidden.astype(jnp.float32) + branch, gain_first, shift_first
    )
    normed_low = normed_first.astype(jnp.bfloat16)
    pre_act = jnp.dot(normed_low, up_full, preferred_element_type=jnp.float32) + up_add
    activated, gelu_pull = jax.vjp(gelu_exact, pre_act)
    activated = activated.astype(jnp.bfloat16)
    ffn_out = jnp.dot(activated, down_full, preferred_element_type=jnp.float32) + down_add
    result, second_pull = jax.vjp(layer_norm, normed_first + ffn_out, gain_second, shift_second)
    again_weights = (
        lax.all_gather(stacked_weight, "shard", axis=0, tiled=True),
        lax.all_gather(out_weight, "shard", axis=0, tiled=True),
        lax.all_gather(up_weight, "shard", axis=0, tiled=True),
        lax.all_gather(down_weight, "shard", axis=0, tiled=True),
    )
    stack_full, out_full, up_full, down_full = (
        again_weights[0],
        again_weights[1],
        again_weights[2],
        again_weights[3],
    )
    second_grad, gain_second_grad, shift_second_grad = second_pull(upstream)
    ffn_grad = second_grad.astype(jnp.bfloat16)
    down_wgrad = jnp.einsum("rf,rd->fd", activated, ffn_grad, preferred_element_type=jnp.float32)
    down_add_grad = jnp.sum(ffn_grad.astype(jnp.float32), 0)
    act_grad = jnp.einsum("rd,fd->rf", ffn_grad, down_full, preferred_element_type=jnp.float32)
    pre_grad = gelu_pull(act_grad)[0].astype(jnp.bfloat16)
    up_wgrad = jnp.einsum("rd,rf->df", normed_low, pre_grad, preferred_element_type=jnp.float32)
    up_add_grad = jnp.sum(pre_grad.astype(jnp.float32), 0)
    normed_grad = second_grad + jnp.einsum(
        "rf,df->rd", pre_grad, up_full, preferred_element_type=jnp.float32
    )
    first_grad, gain_first_grad, shift_first_grad = first_pull(normed_grad)
    branch_grad = first_grad.astype(jnp.bfloat16)
    out_wgrad = jnp.einsum("rd,re->de", attended, branch_grad, preferred_element_type=jnp.float32)
    out_add_grad = jnp.sum(branch_grad.astype(jnp.float32), 0)
    attended_grad = jnp.einsum(
        "re,de->rd", branch_grad, out_full, preferred_element_type=jnp.float32
    ).astype(jnp.bfloat16)
    grad_grp = by_block(attended_grad)

    def backward_group(group_items):
        query_one, key_one, value_one, log_one, grad_one = group_items

        def backward_per_block(running, block_items):
            key_acc, value_acc = running
            query_blk, seg_query, log_total, out_grad = block_items
            scores = masked_scores(query_blk, key_one, seg_query, seg_rows, score_scale)
            prob_full = jnp.exp(scores - log_total)
            value_acc = value_acc + jnp.einsum(
                "hqk,qhd->khd",
                prob_full.astype(jnp.bfloat16),
                out_grad,
                preferred_element_type=jnp.float32,
            )
            prob_grad = jnp.einsum(
                "qhd,khd->hqk", out_grad, value_one, preferred_element_type=jnp.float32
            )
            inner_sum = jnp.sum(prob_full * prob_grad, -1, keepdims=True)
            score_grad = (prob_full * (prob_grad - inner_sum)).astype(jnp.bfloat16)
            query_grad = (
                jnp.einsum("hqk,khd->qhd", score_grad, key_one, preferred_element_type=jnp.float32)
                * score_scale
            )
            key_acc = (
                key_acc
                + jnp.einsum(
                    "hqk,qhd->khd", score_grad, query_blk, preferred_element_type=jnp.float32
                )
                * score_scale
            )
            return ((key_acc, value_acc), query_grad)

        empty_acc = jnp.zeros(key_one.shape, jnp.float32)
        (key_grad, value_grad), query_grads = lax.scan(
            backward_per_block, (empty_acc, empty_acc), (query_one, seg_blocks, log_one, grad_one)
        )
        return (query_grads, key_grad, value_grad)

    query_grads, key_grads, value_grads = lax.map(
        backward_group, (query_grp, key_grp, value_grp, log_totals, grad_grp)
    )
    stacked_rows = jnp.concatenate(
        [from_block(query_grads), from_head(key_grads), from_head(value_grads)], 1
    ).astype(jnp.bfloat16)
    stack_wgrad = jnp.einsum("rd,re->de", hidden, stacked_rows, preferred_element_type=jnp.float32)
    query_add_grad = jnp.sum(stacked_rows[:, :feature_count].astype(jnp.float32), 0)
    value_add_grad = jnp.sum(stacked_rows[:, 2 * feature_count :].astype(jnp.float32), 0)
    input_rows = first_grad + jnp.einsum(
        "re,de->rd", stacked_rows, stack_full, preferred_element_type=jnp.float32
    )
    out_recv, input_recv = (
        lax.all_to_all(
            result.astype(jnp.bfloat16).reshape(dest_count, per_dest, feature_count),
            "shard",
            split_axis=0,
            concat_axis=0,
            tiled=True,
        ),
        lax.all_to_all(
            input_rows.astype(jnp.bfloat16).reshape(dest_count, per_dest, feature_count),
            "shard",
            split_axis=0,
            concat_axis=0,
            tiled=True,
        ),
    )
    layer_out = jnp.take(
        jnp.concatenate([out_recv.reshape(row_count, feature_count), zero_row], 0), landing, axis=0
    )
    input_grad = jnp.take(
        jnp.concatenate([input_recv.reshape(row_count, feature_count), zero_row], 0),
        landing,
        axis=0,
    )
    all_local = (
        lax.psum_scatter(
            stack_wgrad.astype(jnp.bfloat16), "shard", scatter_dimension=0, tiled=True
        ).astype(jnp.float32),
        lax.psum_scatter(
            query_add_grad.astype(jnp.bfloat16), "shard", scatter_dimension=0, tiled=True
        ).astype(jnp.float32),
        lax.psum_scatter(
            value_add_grad.astype(jnp.bfloat16), "shard", scatter_dimension=0, tiled=True
        ).astype(jnp.float32),
        lax.psum_scatter(
            out_wgrad.astype(jnp.bfloat16), "shard", scatter_dimension=0, tiled=True
        ).astype(jnp.float32),
        lax.psum_scatter(
            out_add_grad.astype(jnp.bfloat16), "shard", scatter_dimension=0, tiled=True
        ).astype(jnp.float32),
        lax.psum_scatter(
            gain_first_grad.astype(jnp.bfloat16), "shard", scatter_dimension=0, tiled=True
        ).astype(jnp.float32),
        lax.psum_scatter(
            shift_first_grad.astype(jnp.bfloat16), "shard", scatter_dimension=0, tiled=True
        ).astype(jnp.float32),
        lax.psum_scatter(
            up_wgrad.astype(jnp.bfloat16), "shard", scatter_dimension=0, tiled=True
        ).astype(jnp.float32),
        lax.psum_scatter(
            up_add_grad.astype(jnp.bfloat16), "shard", scatter_dimension=0, tiled=True
        ).astype(jnp.float32),
        lax.psum_scatter(
            down_wgrad.astype(jnp.bfloat16), "shard", scatter_dimension=0, tiled=True
        ).astype(jnp.float32),
        lax.psum_scatter(
            down_add_grad.astype(jnp.bfloat16), "shard", scatter_dimension=0, tiled=True
        ).astype(jnp.float32),
        lax.psum_scatter(
            gain_second_grad.astype(jnp.bfloat16), "shard", scatter_dimension=0, tiled=True
        ).astype(jnp.float32),
        lax.psum_scatter(
            shift_second_grad.astype(jnp.bfloat16), "shard", scatter_dimension=0, tiled=True
        ).astype(jnp.float32),
    )
    all_summed = (
        lax.psum(all_local[0].astype(jnp.bfloat16), "replica").astype(jnp.float32),
        lax.psum(all_local[1].astype(jnp.bfloat16), "replica").astype(jnp.float32),
        lax.psum(all_local[2].astype(jnp.bfloat16), "replica").astype(jnp.float32),
        lax.psum(all_local[3].astype(jnp.bfloat16), "replica").astype(jnp.float32),
        lax.psum(all_local[4].astype(jnp.bfloat16), "replica").astype(jnp.float32),
        lax.psum(all_local[5].astype(jnp.bfloat16), "replica").astype(jnp.float32),
        lax.psum(all_local[6].astype(jnp.bfloat16), "replica").astype(jnp.float32),
        lax.psum(all_local[7].astype(jnp.bfloat16), "replica").astype(jnp.float32),
        lax.psum(all_local[8].astype(jnp.bfloat16), "replica").astype(jnp.float32),
        lax.psum(all_local[9].astype(jnp.bfloat16), "replica").astype(jnp.float32),
        lax.psum(all_local[10].astype(jnp.bfloat16), "replica").astype(jnp.float32),
        lax.psum(all_local[11].astype(jnp.bfloat16), "replica").astype(jnp.float32),
        lax.psum(all_local[12].astype(jnp.bfloat16), "replica").astype(jnp.float32),
    )
    return (
        layer_out,
        input_grad,
        all_summed[0],
        all_summed[1],
        all_summed[2],
        all_summed[3],
        all_summed[4],
        all_summed[5],
        all_summed[6],
        all_summed[7],
        all_summed[8],
        all_summed[9],
        all_summed[10],
        all_summed[11],
        all_summed[12],
    )


def solution(mesh):
    placed = (
        P(("replica", "shard"), None),
        P(("replica", "shard"), None),
        P("replica", None),
        P("replica", None),
        P("replica", None),
        P("shard", None),
        P("shard"),
        P("shard"),
        P("shard", None),
        P("shard"),
        P("shard"),
        P("shard"),
        P("shard", None),
        P("shard"),
        P("shard", None),
        P("shard"),
        P("shard"),
        P("shard"),
    )
    return jax.shard_map(
        shards,
        mesh=mesh,
        in_specs=placed,
        out_specs=(
            P(("replica", "shard"), None),
            P(("replica", "shard"), None),
            P("shard", None),
            P("shard"),
            P("shard"),
            P("shard", None),
            P("shard"),
            P("shard"),
            P("shard"),
            P("shard", None),
            P("shard"),
            P("shard", None),
            P("shard"),
            P("shard"),
            P("shard"),
        ),
        check_vma=False,
    )
```

profile of v0, /device:TPU:9, one launch (start us, length us, event | category | flops | bytes accessed | tf_op | source)
XLA Modules:
  0.0 935.7 jit_solution(13939441732286008834)
XLA Ops:
  28.2 5.9 all-to-all-start
  37.7 72.5 %all-reduce.23 = (bf16[768]{0:T(1024)(128)(2,1)S(1)}, bf16[768]{0:T(1024)(128)(2,1)S(1)}, bf16[768]{0:T(1024)(128)(2,1)S(1)}, bf16[768]{0:T(1024)(128)(2,1)S(1)}...) all-reduce(bf16[768]{0:T(1024)(128)(2,1)S(1)} %dynamic-update-slice, ...), channel_id=1, replica_groups=mesh['replica'=4,'shard'=8] {'shard'}, use_global_device_ids=true, to_apply=%add.6 | all-reduce | flops 5376 | bytes 21504
  112.0 22.7 %all-gather = bf16[8,1,384]{2,1,0:T(2,128)(2,1)S(1)} all-gather(bf16[1,1,384]{2,1,0:T(2,128)(2,1)S(1)} %reshape.369), channel_id=1, replica_groups=mesh['replica'=4,'shard'=8] {'shard'}, dimensions={0}, use_global_device_ids=true | all-gather | bytes 6912 | tf_op jit(solution)/shard_map/all_gather | solution.py:123
  136.7 6.2 all-to-all-start.2
  143.1 6.0 add_convert_fusion.1
  163.3 52.6 %while.58 = (s32[]{:T(128)}, bf16[3,2,512,4,64]{2,4,3,1,0:T(8,128)(2,1)}, f32[3,2,4,512,1]{3,2,1,4,0:T(4,128)}, bf16[3,2,512,4,64]{2,4,3,1,0:T(8,128)(2,1)}, bf1...) while((s32[]{:T(128)}, ...), condition=%wide.region_7.9_spmd.clone, body=%wide.region_2.8_spmd.clone.sunk | while | flops 560592896 | bytes 33150768 | solution.py:189
  165.8 13.5 %while.61 = (s32[]{:T(128)}, bf16[2,512,4,64]{1,3,2,0:T(8,128)(2,1)S(1)}, f32[2,4,512,1]{2,1,3,0:T(4,128)S(1)}, s32[2,512]{1,0:T(2,128)S(1)}, s32[8,128]{1,0:T(8...) while((s32[]{:T(128)}, ...), condition=%wide.region_6.7_spmd, body=%wide.region_3.6_spmd.sunk | while | flops 560592896 | bytes 28911724 | solution.py:187
  183.2 13.5 %while.61 = (s32[]{:T(128)}, bf16[2,512,4,64]{1,3,2,0:T(8,128)(2,1)S(1)}, f32[2,4,512,1]{2,1,3,0:T(4,128)S(1)}, s32[2,512]{1,0:T(2,128)S(1)}, s32[8,128]{1,0:T(8...) while((s32[]{:T(128)}, ...), condition=%wide.region_6.7_spmd, body=%wide.region_3.6_spmd.sunk | while | flops 560592896 | bytes 28911724 | solution.py:187
  200.7 13.5 %while.61 = (s32[]{:T(128)}, bf16[2,512,4,64]{1,3,2,0:T(8,128)(2,1)S(1)}, f32[2,4,512,1]{2,1,3,0:T(4,128)S(1)}, s32[2,512]{1,0:T(2,128)S(1)}, s32[8,128]{1,0:T(8...) while((s32[]{:T(128)}, ...), condition=%wide.region_6.7_spmd, body=%wide.region_3.6_spmd.sunk | while | flops 560592896 | bytes 28911724 | solution.py:187
  225.0 16.8 %all-gather.10.cloned.1.call-done = bf16[768,3072]{1,0:T(8,128)(2,1)} async-done(((bf16[96,3072]{1,0:T(8,128)(2,1)}), bf16[768,3072]{1,0:T(8,128)(2,1)}) %all-gather.10.cloned.1.call-update) | async-done | bytes 4718608 | tf_op jit(solution)/shard_map/all_gather | solution.py:116
  241.8 35.8 %multiply_convert_fusion.1 = (bf16[1024,3072]{1,0:T(8,128)(2,1)}, f32[1024,3072]{1,0:T(8,128)}, f32[1024,3072]{1,0:T(8,128)}) fusion(f32[3072]{0:T(1024)S(1)} %bitcast.307, bf16[768,3072]{1,0:T(8,128)(2,1)} %all-gather.10.cloned.1.call-done, f32[1024,768]{1,0:T(8,128)S(1)} %get-tuple-element.531, f32[768]{0:T(1024)S(1)} %copy-done.46, ...), kind=kOutput, calls=%fused_computation.77 | convolution fusion | flops 5043388416 | bytes 39348224 | tf_op jit(solution)/shard_map/dot_general | solution.py:196
  277.6 44.3 %all-gather.12.cloned.1.call-done = bf16[3072,768]{1,0:T(8,128)(2,1)} async-done(((bf16[384,768]{1,0:T(8,128)(2,1)}), bf16[3072,768]{1,0:T(8,128)(2,1)}) %all-gather.12.cloned.1.call-update) | async-done | bytes 4718608 | tf_op jit(solution)/shard_map/all_gather | solution.py:117
  321.9 9.7 %fusion.85 = (f32[1024]{0:T(1024)S(1)}, f32[1024,768]{1,0:T(8,128)S(1)}) fusion(f32[768]{0:T(1024)S(1)} %copy-done.48, bf16[1024,3072]{1,0:T(8,128)(2,1)} %get-tuple-element.510, bf16[3072,768]{1,0:T(8,128)(2,1)} %all-gather.12.cloned.1.call-done, f32[768]{0:T(1024)S(1)} %copy-done.46, f32[768]{0:T(1024)S(1)} %copy-done.34, f32[1024]{0:T(1024)S(1)} %fusion.68, ...), kind=kOutput, calls=%fused_computation.189 | convolution fusion | flops 4837342208 | bytes 17323008 | tf_op jit(solution)/shard_map/dot_general | solution.py:199
  340.6 19.0 %fusion.86 = (bf16[3072]{0:T(1024)(128)(2,1)}, bf16[1024,3072]{1,0:T(8,128)(2,1)}) fusion(f32[1024,3072]{1,0:T(8,128)} %get-tuple-element.511, bf16[1024,768]{1,0:T(8,128)(2,1)} %get-tuple-element.503, bf16[3072,768]{1,0:T(8,128)(2,1)} %all-gather.12.cloned.1.call-done, f32[1024,3072]{1,0:T(8,128)} %get-tuple-element.532, f32[3072]{0:T(1024)S(1)} %bitcast.308), kind=kOutput, calls=%fused_computation.190 | convolution fusion | flops 4882166784 | bytes 37767168 | tf_op jit(solution)/shard_map/rd,fd->rf/dot_general | solution.py:217
  359.6 10.2 %multiply_reduce_fusion.1 = (bf16[768]{0:T(1024)(128)(2,1)}, f32[1024]{0:T(1024)S(1)}, bf16[768]{0:T(1024)(128)(2,1)}, f32[1024,768]{1,0:T(8,128)S(1)}) fusion(f32[1024,768]{1,0:T(8,128)S(1)} %copy-done.7, f32[1024]{0:T(1024)S(1)} %fusion.68, f32[1024]{0:T(1024)S(1)} %broadcast_multiply_fusion.1, f32[768]{0:T(1024)S(1)} %copy-done.34, ...), kind=kOutput, calls=%fused_computation.104 | convolution fusion | flops 4839699456 | bytes 20469760 | tf_op jit(solution)/shard_map/rf,df->rd/dot_general | solution.py:221
  382.0 153.5 %while.60 = (s32[]{:T(128)}, bf16[3,2,512,4,64]{2,4,3,1,0:T(8,128)(2,1)}, bf16[3,1024,4,64]{1,3,2,0:T(8,128)(2,1)}, bf16[3,1024,4,64]{1,3,2,0:T(8,128)(2,1)}, bf...) while((s32[]{:T(128)}, ...), condition=%wide.region_24.26_spmd.clone, body=%wide.region_20.25_spmd.clone.sunk | while | flops 1375598592 | bytes 166836848 | solution.py:271
  387.4 41.5 %while.62 = (s32[]{:T(128)}, f32[1024,4,64]{0,2,1:T(8,128)S(1)}, f32[1024,4,64]{0,2,1:T(8,128)}, bf16[2,512,4,64]{1,3,2,0:T(8,128)(2,1)}, bf16[2,512,4,64]{1,3,2...) while((s32[]{:T(128)}, f32[1024,4,64]{0,2,1:T(8,128)S(1)}, ...), condition=%wide.region_23.24_spmd.clone, body=%wide.region_21.23_spmd.clone.sunk | while | flops 1375598592 | bytes 143723280 | solution.py:266
  438.6 41.4 %while.62 = (s32[]{:T(128)}, f32[1024,4,64]{0,2,1:T(8,128)S(1)}, f32[1024,4,64]{0,2,1:T(8,128)}, bf16[2,512,4,64]{1,3,2,0:T(8,128)(2,1)}, bf16[2,512,4,64]{1,3,2...) while((s32[]{:T(128)}, f32[1024,4,64]{0,2,1:T(8,128)S(1)}, ...), condition=%wide.region_23.24_spmd.clone, body=%wide.region_21.23_spmd.clone.sunk | while | flops 1375598592 | bytes 143723280 | solution.py:266
  489.6 41.4 %while.62 = (s32[]{:T(128)}, f32[1024,4,64]{0,2,1:T(8,128)S(1)}, f32[1024,4,64]{0,2,1:T(8,128)}, bf16[2,512,4,64]{1,3,2,0:T(8,128)(2,1)}, bf16[2,512,4,64]{1,3,2...) while((s32[]{:T(128)}, f32[1024,4,64]{0,2,1:T(8,128)S(1)}, ...), condition=%wide.region_23.24_spmd.clone, body=%wide.region_21.23_spmd.clone.sunk | while | flops 1375598592 | bytes 143723280 | solution.py:266
  540.3 8.5 convolution_convert_fusion.2
  550.2 9.7 %convolution_convert_fusion = bf16[3072,768]{1,0:T(8,128)(2,1)} fusion(bf16[1024,3072]{1,0:T(8,128)(2,1)} %get-tuple-element.510, bf16[1024,768]{1,0:T(8,128)(2,1)S(1)} %copy-done.14), kind=kOutput, calls=%fused_computation.92 | convolution fusion | flops 4834197504 | bytes 12582912 | tf_op jit(solution)/shard_map/rf,rd->fd/dot_general | solution.py:215
  561.9 10.0 %convolution_convert_fusion.1 = bf16[768,3072]{1,0:T(8,128)(2,1)} fusion(bf16[1024,3072]{1,0:T(8,128)(2,1)} %get-tuple-element.537, f32[1024,768]{1,0:T(8,128)S(1)} %copy-done.8, f32[768]{0:T(1024)S(1)} %copy-done.47, f32[768]{0:T(1024)S(1)} %copy-done.35, f32[1024]{0:T(1024)S(1)} %copy-done.37, f32[1024]{0:T(1024)S(1)} %copy-done.33), kind=kOutput, calls=%fused_computation.93 | convolution fusion | flops 4838129664 | bytes 14170112 | tf_op jit(solution)/shard_map/rd,rf->df/dot_general | solution.py:219
  578.3 27.3 %all-reduce.22 = (bf16[768]{0:T(1024)(128)(2,1)S(1)}, bf16[768]{0:T(1024)(128)(2,1)S(1)}, bf16[768]{0:T(1024)(128)(2,1)S(1)}, bf16[768]{0:T(1024)(128)(2,1)S(1)}...) all-reduce(bf16[768]{0:T(1024)(128)(2,1)S(1)} %dynamic-update-slice, ...), channel_id=1, replica_groups=mesh['replica'=4,'shard'=8] {'shard'}, use_global_device_ids=true, to_apply=%add.12 | all-reduce | flops 9984 | bytes 39936
  607.4 7.4 all-to-all-start.1
  614.9 8.7 add_convert_fusion.2
  623.5 42.4 %all-to-all-done.1 = bf16[8,128,768]{2,1,0:T(8,128)(2,1)} async-done(((bf16[8,128,768]{2,1,0:T(8,128)(2,1)}), bf16[8,128,768]{2,1,0:T(8,128)(2,1)}, u32[]{:S(2)}, u32[]{:S(2)}) %all-to-all-start.1) | async-done | bytes 1572896 | tf_op jit(solution)/shard_map/all_to_all | solution.py:284
  665.9 8.5 all-to-all-start.3
  674.7 100.4 %reduce-scatter.11.cloned.1.call-done = bf16[384,768]{1,0:T(8,128)(2,1)} async-done(((bf16[3072,768]{1,0:T(8,128)(2,1)}), bf16[384,768]{1,0:T(8,128)(2,1)}) %reduce-scatter.11.cloned.1.call-update) | async-done | bytes 589840 | tf_op jit(solution)/shard_map/reduce_scatter | solution.py:335
  775.0 98.9 %reduce-scatter.9.cloned.1.call-done = bf16[96,3072]{1,0:T(8,128)(2,1)} async-done(((bf16[768,3072]{1,0:T(8,128)(2,1)}), bf16[96,3072]{1,0:T(8,128)(2,1)}) %reduce-scatter.9.cloned.1.call-update) | async-done | bytes 589840 | tf_op jit(solution)/shard_map/reduce_scatter | solution.py:329
  876.0 5.9 all-reduce.24
  888.2 5.2 gather_fusion.1
  902.2 20.6 %all-reduce.28.cloned.1.call-done = (bf16[96,2304]{1,0:T(8,128)(2,1)}, bf16[96,768]{1,0:T(8,128)(2,1)}, bf16[96,3072]{1,0:T(8,128)(2,1)}, bf16[384,768]{1,0:T(8,128)(2,1)}) async-done(((bf16[96,2304]{1,0:T(8,128)(2,1)}, bf16[96,768]{1,0:T(8,128)(2,1)}, bf16[96,3072]{1,0:T(8,128)(2,1)}, bf16[384,768]{1,0:T(8,128)(2,1)}), (bf16[96,2304]{1,0:T(8,128)(2,1)}, bf16[96,768]{1,0:T(8,128)(2,1)}, ...) | async-done | bytes 1769488 | tf_op jit(solution)/shard_map/psum | solution.py:349
  (480 shorter events, 314.8 us)
Async XLA Ops:
  7.2 135.9 %all-gather.6.cloned.1.call-start = ((), (), s32[]{:S(2)}) async-start(), calls=%async_computation.8 | async-start | bytes 3981312 | tf_op jit(solution)/shard_map/all_gather | solution.py:114
  7.9 212.6 %all-gather.8.cloned.1.call-start = ((), (), s32[]{:S(2)}) async-start(), calls=%async_computation.9 | async-start | bytes 1327104 | tf_op jit(solution)/shard_map/all_gather | solution.py:115
  8.7 233.1 %all-gather.10.cloned.1.call-start = ((), (), s32[]{:S(2)}) async-start(), calls=%async_computation.10 | async-start | bytes 5308416 | tf_op jit(solution)/shard_map/all_gather | solution.py:116
  28.2 9.2 copy-start.64
  28.2 83.8 %copy-start.53 = (bf16[384]{0:T(512)(128)(2,1)S(1)}, bf16[384]{0:T(512)(128)(2,1)}, u32[]{:S(2)}) copy-start(bf16[384]{0:T(512)(128)(2,1)} %param.41) | copy-start | bytes 2308
  28.2 108.4 %all-to-all-start = ((bf16[8,128,768]{2,1,0:T(8,128)(2,1)}), bf16[8,128,768]{2,1,0:T(8,128)(2,1)S(1)}, u32[]{:S(2)}, u32[]{:S(2)}) async-start(bf16[8,128,768]{2,1,0:T(8,128)(2,1)} %bitcast.15), calls=%async_computation | async-start | bytes 3145728 | tf_op jit(solution)/shard_map/all_to_all | solution.py:93
  34.1 287.8 %all-gather.12.cloned.1.call-start = ((), (), s32[]{:S(2)}) async-start(), calls=%async_computation.11 | async-start | bytes 5308416 | tf_op jit(solution)/shard_map/all_gather | solution.py:117
  136.7 195.5 %all-to-all-start.2 = ((bf16[8,128,768]{2,1,0:T(8,128)(2,1)}), bf16[8,128,768]{2,1,0:T(8,128)(2,1)}, u32[]{:S(2)}, u32[]{:S(2)}) async-start(bf16[8,128,768]{2,1,0:T(8,128)(2,1)} %bitcast.29), calls=%async_computation.2 | async-start | bytes 3145728 | tf_op jit(solution)/shard_map/all_to_all | solution.py:100
  142.9 531.8 %reduce-scatter.7.cloned.1.call-start = ((), (), s32[]{:S(2)}) async-start(), calls=%async_computation.13 | async-start | bytes 1327104 | tf_op jit(solution)/shard_map/reduce_scatter | solution.py:317
  224.4 53.2 %copy-start.6 = (f32[1024,768]{1,0:T(8,128)}, f32[1024,768]{1,0:T(8,128)S(1)}, u32[]{:S(2)}) copy-start(f32[1024,768]{1,0:T(8,128)S(1)} %get-tuple-element.531) | copy-start | bytes 9437188
  224.5 17.3 %copy-start.34 = (f32[768]{0:T(1024)S(1)}, f32[768]{0:T(1024)}, u32[]{:S(2)}) copy-start(f32[768]{0:T(1024)} %convert_element_type.183) | copy-start | bytes 9220
  224.5 17.3 %copy-start.40 = (f32[8,1,384]{2,1,0:T(1,128)S(1)}, f32[8,1,384]{2,1,0:T(1,128)}, u32[]{:S(2)}) copy-start(f32[8,1,384]{2,1,0:T(1,128)} %convert_element_type.220) | copy-start | bytes 36868
  224.5 17.3 %copy-start.46 = (f32[768]{0:T(1024)S(1)}, f32[768]{0:T(1024)}, u32[]{:S(2)}) copy-start(f32[768]{0:T(1024)} %convert_element_type.184) | copy-start | bytes 9220
  224.5 145.3 %copy-start.32 = (f32[1024]{0:T(1024)}, f32[1024]{0:T(1024)S(1)}, u32[]{:S(2)}) copy-start(f32[1024]{0:T(1024)S(1)} %broadcast_multiply_fusion.1) | copy-start | bytes 12292
  225.0 144.7 %copy-start.36 = (f32[1024]{0:T(1024)}, f32[1024]{0:T(1024)S(1)}, u32[]{:S(2)}) copy-start(f32[1024]{0:T(1024)S(1)} %fusion.68) | copy-start | bytes 12292
  241.8 80.1 %copy-start.48 = (f32[768]{0:T(1024)S(1)}, f32[768]{0:T(1024)}, u32[]{:S(2)}) copy-start(f32[768]{0:T(1024)} %convert_element_type.188) | copy-start | bytes 9220
  340.6 19.0 %copy-start.7 = (f32[1024,768]{1,0:T(8,128)S(1)}, f32[1024,768]{1,0:T(8,128)}, u32[]{:S(2)}) copy-start(f32[1024,768]{1,0:T(8,128)} %copy-done.6) | copy-start | bytes 9437188
  376.3 298.3 %reduce-scatter.5.cloned.1.call-start = ((), (), s32[]{:S(2)}) async-start(), calls=%async_computation.12 | async-start | bytes 3981312 | tf_op jit(solution)/shard_map/reduce_scatter | solution.py:308
  548.8 226.2 %reduce-scatter.11.cloned.1.call-start = ((), (), s32[]{:S(2)}) async-start(), calls=%async_computation.15 | async-start | bytes 5308416 | tf_op jit(solution)/shard_map/reduce_scatter | solution.py:335
  560.0 313.9 %reduce-scatter.9.cloned.1.call-start = ((), (), s32[]{:S(2)}) async-start(), calls=%async_computation.14 | async-start | bytes 5308416 | tf_op jit(solution)/shard_map/reduce_scatter | solution.py:329
  571.9 33.7 %copy-start.5 = (f32[1024,768]{1,0:T(8,128)S(1)}, f32[1024,768]{1,0:T(8,128)}, u32[]{:S(2)}) copy-start(f32[1024,768]{1,0:T(8,128)} %copy-done.4) | copy-start | bytes 9437188
  571.9 33.7 %copy-start.25 = (f32[1024]{0:T(1024)S(1)}, f32[1024]{0:T(1024)}, u32[]{:S(2)}) copy-start(f32[1024]{0:T(1024)} %copy-done.24) | copy-start | bytes 12292
  572.0 33.7 %copy-start.27 = (f32[768]{0:T(1024)S(1)}, f32[768]{0:T(1024)}, u32[]{:S(2)}) copy-start(f32[768]{0:T(1024)} %convert_element_type.189) | copy-start | bytes 9220
  572.0 33.7 %copy-start.29 = (f32[1024]{0:T(1024)S(1)}, f32[1024]{0:T(1024)}, u32[]{:S(2)}) copy-start(f32[1024]{0:T(1024)} %copy-done.28) | copy-start | bytes 12292
  605.7 9.2 copy-start.39
  607.4 58.5 %all-to-all-start.1 = ((bf16[8,128,768]{2,1,0:T(8,128)(2,1)}), bf16[8,128,768]{2,1,0:T(8,128)(2,1)}, u32[]{:S(2)}, u32[]{:S(2)}) async-start(bf16[8,128,768]{2,1,0:T(8,128)(2,1)} %bitcast.291), calls=%async_computation.1 | async-start | bytes 3145728 | tf_op jit(solution)/shard_map/all_to_all | solution.py:284
  623.5 50.9 %copy-start.45 = (s32[1,16]{1,0:T(1,128)S(1)}, s32[1,16]{1,0:T(1,128)}, u32[]{:S(2)}) copy-start(s32[1,16]{1,0:T(1,128)} %param.32) | copy-start | bytes 196
  623.5 50.9 %copy-start.66 = (s32[1,16]{1,0:T(1,128)S(1)}, s32[1,16]{1,0:T(1,128)}, u32[]{:S(2)}) copy-start(s32[1,16]{1,0:T(1,128)} %param.30) | copy-start | bytes 196
  623.5 50.9 %copy-start.54 = (s32[16]{0:T(128)S(1)}, s32[16]{0:T(128)}, u32[]{:S(2)}) copy-start(s32[16]{0:T(128)} %get-tuple-element.391) | copy-start | bytes 196
  623.5 50.9 %copy-start.55 = (s32[16]{0:T(128)S(1)}, s32[16]{0:T(128)}, u32[]{:S(2)}) copy-start(s32[16]{0:T(128)} %get-tuple-element.392) | copy-start | bytes 196
  665.9 227.5 %all-to-all-start.3 = ((bf16[8,128,768]{2,1,0:T(8,128)(2,1)}), bf16[8,128,768]{2,1,0:T(8,128)(2,1)S(1)}, u32[]{:S(2)}, u32[]{:S(2)}) async-start(bf16[8,128,768]{2,1,0:T(8,128)(2,1)} %bitcast.300), calls=%async_computation.3 | async-start | bytes 3145728 | tf_op jit(solution)/shard_map/all_to_all | solution.py:291
  674.4 248.4 %all-reduce.28.cloned.1.call-start = ((), (), s32[]{:S(2)}) async-start(), calls=%async_computation.16 | async-start | bytes 3538944 | tf_op jit(solution)/shard_map/psum | solution.py:349
  (72 other events, 321.6 us)
Sparse Core Ops, SparseCore 0:
  10.2 89.6 all-gather.5
  102.1 39.3 all-gather.7
  143.7 98.0 all-gather.9
  243.8 78.0 all-gather.11
  376.4 62.0 reduce-scatter.6
  549.0 86.7 reduce-scatter.4
  639.4 135.5 reduce-scatter.10
  778.7 95.1 reduce-scatter.8
  876.5 46.2 all-reduce.27
where the time goes:
time: 944 us; the launch traced here: 936 us
  waiting for transfers between devices  326 us (35%)
  matrix products  250 us (26%)
  blocking collectives  129 us (14%)
  local copies, waits for them, and re-layouts  101 us (11%)
  other arithmetic  83.6 us (9%)
  starting transfers between devices  28.6 us (3%)
  between operations  17 us (2%)
    reduce_scatter x1, waiting for transfers between devices, shards(): lax.psum_scatter(down_wgrad.astype(jnp.bfloat16), 'shard', scatter_dimens...  100 us
    unnamed x2, blocking collectives  99.9 us
    reduce_scatter x1, waiting for transfers between devices, shards(): lax.psum_scatter(up_wgrad.astype(jnp.bfloat16), 'shard', scatter_dimensio...  98.9 us
    all_gather x1, waiting for transfers between devices, shards(): lax.all_gather(down_weight, 'shard', axis=0, tiled=True)  44.3 us
    all_to_all x1, waiting for transfers between devices, shards(): lax.all_to_all(result.astype(jnp.bfloat16).reshape(dest_count, per_dest,...  42.4 us
    dot_general x1, matrix products, shards(): jnp.dot(normed_low, up_full, preferred_element_type=jnp.float32) + up_add  35.8 us
    dot_general x6, matrix products, backward_per_block(): jnp.einsum('hqk,khd->qhd', score_grad, key_one, preferred_element_type=jn...  28 us
    dot_general x6, matrix products, backward_per_block(): jnp.einsum('hqk,qhd->khd', prob_full.astype(jnp.bfloat16), out_grad, pref...  24.5 us
  transfers between devices with their start and end apart: 13, of which 6 were waited for; matrix products, arithmetic and copies ran while one was open for 40% of the time, Pallas kernels for 0%

commit v1 on v0

v1 whole, which is shorter than its diff:
```python
import functools
import math

import jax
import jax.numpy as jnp
from jax import lax
from jax.experimental import pallas as pl
from jax.experimental.pallas import tpu as pltpu
from jax.sharding import PartitionSpec as P

HEADS = 12
HEAD_DIM = 64
EPSILON = 1e-12
PENALTY = -(2.0**30)
LANES = 128
SMALL_ROWS = 16

BF = jnp.bfloat16
F32 = jnp.float32


def dot(a, b):
    return jnp.dot(a, b, preferred_element_type=F32)


def dot_nt(a, b):
    return lax.dot_general(a, b, (((1,), (1,)), ((), ())), preferred_element_type=F32)


def dot_tn(a, b):
    return lax.dot_general(a, b, (((0,), (0,)), ((), ())), preferred_element_type=F32)


def routing(lengths, deal_order, starts, row_count, dest_count):
    total_seqs = lengths.shape[0]
    per_dest = row_count // dest_count
    labels = jnp.arange(total_seqs, dtype=jnp.int32)
    chosen = (deal_order[:, None] == labels[None, :]).astype(jnp.int32)
    dealt_len = jnp.sum(chosen * lengths[None, :], 1).reshape(dest_count, 2)
    dealt_start = jnp.sum(chosen * starts[None, :], 1).reshape(dest_count, 2)
    first_len = dealt_len[:, 0:1]
    second_len = dealt_len[:, 1:2]
    position = jnp.arange(per_dest, dtype=jnp.int32)[None, :]
    in_first = position < first_len
    in_second = jnp.logical_and(position >= first_len, position < first_len + second_len)
    source_rows = jnp.where(
        in_first,
        dealt_start[:, 0:1] + position,
        jnp.where(in_second, dealt_start[:, 1:2] + position - first_len, row_count),
    )
    segments = jnp.where(in_first, 0, jnp.where(in_second, 1, 2)).astype(jnp.int32)
    placed = jnp.sum(chosen * labels[:, None], 0)
    earlier = jnp.concatenate([jnp.zeros((dest_count, 1), jnp.int32), first_len], 1).reshape(-1)
    offset = placed // 2 * per_dest + jnp.sum(chosen * earlier[:, None], 0)
    row_index = jnp.arange(row_count, dtype=jnp.int32)[:, None]
    member = jnp.logical_and(row_index >= starts[None, :], row_index < (starts + lengths)[None, :])
    landing = jnp.sum(jnp.where(member, offset[None, :] + row_index - starts[None, :], 0), 1)
    landing = landing + jnp.where(jnp.any(member, 1), 0, dest_count * per_dest)
    return (source_rows, segments, landing)


def pick_kernel(rows_ref, values_ref, out_ref):
    wanted = rows_ref[...]
    columns = lax.broadcasted_iota(jnp.int32, (wanted.shape[0], values_ref.shape[0]), 1)
    chosen = jnp.where(columns == wanted, 1.0, 0.0).astype(BF)
    out_ref[...] = dot(chosen, values_ref[...]).astype(BF)


def pick_rows(values, rows):
    count, width = values.shape
    block = min(256, count)
    return pl.pallas_call(
        pick_kernel,
        grid=(count // block,),
        in_specs=[
            pl.BlockSpec((block, 1), lambda i: (i, 0)),
            pl.BlockSpec((count, width), lambda i: (0, 0)),
        ],
        out_specs=pl.BlockSpec((block, width), lambda i: (i, 0)),
        out_shape=jax.ShapeDtypeStruct((count, width), BF),
        cost_estimate=pl.CostEstimate(
            flops=2 * count * count * width, bytes_accessed=4 * count * width, transcendentals=0
        ),
        name="pick_rows",
    )(rows.reshape(count, 1), values)


def attend_kernel(q_ref, k_ref, v_ref, augq_ref, augk_ref, out_ref, aug_ref, kcat, vcat):
    rows = q_ref.shape[0]
    chunk = min(256, rows)
    lane = lax.broadcasted_iota(jnp.int32, (chunk, LANES), 1)
    low = lane < HEAD_DIM
    kcat[:, :LANES] = k_ref[...]
    kcat[:, LANES:] = augk_ref[...]
    vcat[:, :LANES] = v_ref[...]
    vcat[:, LANES:] = jnp.ones((rows, LANES), BF)
    scale = 1.0 / math.sqrt(HEAD_DIM)

    def one_chunk(i):
        here = pl.ds(i * chunk, chunk)
        q = q_ref[here, :] * scale
        seg = augq_ref[here, :]
        mixed = None
        aug = seg.astype(F32)
        for h in range(2):
            mine = low if h == 0 else jnp.logical_not(low)
            qcat = jnp.concatenate([jnp.where(mine, q, jnp.zeros_like(q)), seg], 1)
            scores = dot_nt(qcat, kcat[...])
            peak = jnp.max(scores, 1, keepdims=True)
            probs = jnp.exp(scores - peak).astype(BF)
            acc = dot(probs, vcat[...])
            total = acc[:, LANES:]
            part = acc[:, :LANES] / total
            mixed = part if h == 0 else jnp.where(low, mixed, part)
            lse = peak + jnp.log(total)
            high = lse.astype(BF).astype(F32)
            middle = (lse - high).astype(BF).astype(F32)
            rest = lse - high - middle
            base = 3 + 3 * h
            aug = jnp.where(lane == base, high, aug)
            aug = jnp.where(lane == base + 1, middle, aug)
            aug = jnp.where(lane == base + 2, rest, aug)
        out_ref[here, :] = mixed.astype(BF)
        aug_ref[here, :] = aug.astype(BF)

    for i in range(rows // chunk):
        one_chunk(i)


def attend(qkv, augq, augk):
    rows = qkv.shape[0]
    width = qkv.shape[1] // 3
    pairs = width // LANES
    whole = pl.BlockSpec((rows, LANES), lambda p: (0, 0))
    return pl.pallas_call(
        attend_kernel,
        grid=(pairs,),
        in_specs=[
            pl.BlockSpec((rows, LANES), lambda p: (0, p)),
            pl.BlockSpec((rows, LANES), lambda p: (0, pairs + p)),
            pl.BlockSpec((rows, LANES), lambda p: (0, 2 * pairs + p)),
            whole,
            whole,
        ],
        out_specs=[
            pl.BlockSpec((rows, LANES), lambda p: (0, p)),
            pl.BlockSpec((rows, LANES), lambda p: (0, p)),
        ],
        out_shape=[
            jax.ShapeDtypeStruct((rows, width), BF),
            jax.ShapeDtypeStruct((rows, width), BF),
        ],
        scratch_shapes=[pltpu.VMEM((rows, 2 * LANES), BF), pltpu.VMEM((rows, 2 * LANES), BF)],
        cost_estimate=pl.CostEstimate(
            flops=16 * rows * rows * width,
            bytes_accessed=10 * rows * width,
            transcendentals=rows * rows * HEADS,
        ),
        name="attend",
    )(qkv, qkv, qkv, augq, augk)


def attend_back_kernel(
    q_ref, k_ref, v_ref, aug_ref, augk_ref, a_ref, da_ref,
    dq_ref, dk_ref, dv_ref, qcat, dcat, kt, dqt,
):
    rows = q_ref.shape[0]
    chunk = min(256, rows)
    scale = 1.0 / math.sqrt(HEAD_DIM)
    lane = lax.broadcasted_iota(jnp.int32, (rows, LANES), 1)
    low = lane < HEAD_DIM
    q = q_ref[...] * scale
    grad = da_ref[...]
    aug = aug_ref[...]
    weighted = a_ref[...].astype(F32) * grad.astype(F32)
    zero = jnp.zeros_like(q)
    for h in range(2):
        mine = low if h == 0 else jnp.logical_not(low)
        other = 6 - 3 * h
        skip = jnp.logical_and(lane >= other, lane < other + 3)
        qcat[h, :, :LANES] = jnp.where(mine, q, zero)
        qcat[h, :, LANES:] = jnp.where(skip, zero, aug)
        inner = jnp.sum(jnp.where(mine, weighted, 0.0), 1, keepdims=True)
        high = inner.astype(BF).astype(F32)
        middle = (inner - high).astype(BF).astype(F32)
        rest = inner - high - middle
        split = jnp.where(lane == 0, high, jnp.where(lane == 1, middle, jnp.where(lane == 2, rest, 0.0)))
        dcat[h, :, :LANES] = jnp.where(mine, grad, zero)
        dcat[h, :, LANES:] = split.astype(BF)
    kt[...] = k_ref[...].T
    keyed = lax.broadcasted_iota(jnp.int32, (chunk, LANES), 1)
    minus = jnp.where(keyed < 3, -1.0, 0.0).astype(BF)
    low_key = keyed < HEAD_DIM
    for i in range(rows // chunk):
        here = pl.ds(i * chunk, chunk)
        kcat = jnp.concatenate([k_ref[here, :], augk_ref[here, :]], 1)
        vcat = jnp.concatenate([v_ref[here, :], minus], 1)
        keys = values = None
        for h in range(2):
            probs = jnp.exp(dot_nt(kcat, qcat[h]))
            slopes = dot_nt(vcat, dcat[h])
            low_probs = probs.astype(BF)
            low_slopes = (probs * slopes).astype(BF)
            dv = dot(low_probs, da_ref[...])
            dk = dot(low_slopes, q_ref[...])
            values = dv if h == 0 else jnp.where(low_key, values, dv)
            keys = dk if h == 0 else jnp.where(low_key, keys, dk)
            lines = pl.ds(h * HEAD_DIM, HEAD_DIM)
            part = dot(kt[lines, here], low_slopes)
            if i == 0:
                dqt[lines, :] = part
            else:
                dqt[lines, :] += part
        dv_ref[here, :] = values.astype(BF)
        dk_ref[here, :] = (keys * scale).astype(BF)
    dq_ref[...] = (dqt[...] * scale).T.astype(BF)


def attend_back(qkv, aug, augk, mixed, grad):
    rows = qkv.shape[0]
    width = qkv.shape[1] // 3
    pairs = width // LANES
    whole = pl.BlockSpec((rows, LANES), lambda p: (0, 0))
    mine = pl.BlockSpec((rows, LANES), lambda p: (0, p))
    return pl.pallas_call(
        attend_back_kernel,
        grid=(pairs,),
        in_specs=[
            mine,
            pl.BlockSpec((rows, LANES), lambda p: (0, pairs + p)),
            pl.BlockSpec((rows, LANES), lambda p: (0, 2 * pairs + p)),
            mine,
            whole,
            mine,
            mine,
        ],
        out_specs=[mine, mine, mine],
        out_shape=[jax.ShapeDtypeStruct((rows, width), BF)] * 3,
        scratch_shapes=[
            pltpu.VMEM((2, rows, 2 * LANES), BF),
            pltpu.VMEM((2, rows, 2 * LANES), BF),
            pltpu.VMEM((LANES, rows), BF),
            pltpu.VMEM((LANES, rows), F32),
        ],
        cost_estimate=pl.CostEstimate(
            flops=40 * rows * rows * width,
            bytes_accessed=18 * rows * width,
            transcendentals=rows * rows * HEADS,
        ),
        name="attend_back",
    )(qkv, qkv, qkv, aug, augk, mixed, grad)


def core_swap(x):
    size = lax.axis_size("replica")
    return lax.ppermute(x, "replica", [(r, r ^ 1) for r in range(size)])


def side_swap(x):
    size = lax.axis_size("replica")
    return lax.ppermute(x, "replica", [(r, r ^ 2) for r in range(size)])


def put(buffer, block, index, axis):
    starts = [jnp.int32(0)] * buffer.ndim
    starts[axis] = index
    return lax.dynamic_update_slice(buffer, jnp.expand_dims(block, axis), starts)


def spread(mine):
    rows, width = mine.shape
    half = rows // 2
    shards = lax.axis_size("shard")
    outer = shards // 2
    core = lax.axis_index("replica") % 2
    place = lax.axis_index("shard")
    near, far = place % 2, place // 2
    own = lax.dynamic_slice(mine, (core * half, 0), (half, width))
    line = put(jnp.zeros((outer, half, width), BF), own, far, 0)
    for k in range(1, outer):
        got = lax.ppermute(own, "shard", [(s, s ^ (2 * k)) for s in range(shards)])
        line = put(line, got, far ^ k, 0)
    got = lax.ppermute(line, "shard", [(s, s ^ 1) for s in range(shards)])
    plane = jnp.zeros((outer, 2, half, width), BF)
    plane = put(put(plane, line, near, 1), got, 1 - near, 1)
    got = core_swap(plane)
    full = jnp.zeros((outer, 2, 2, half, width), BF)
    full = put(put(full, plane, core, 2), got, 1 - core, 2)
    return full.reshape(shards, rows, width)


def share_sum(terms):
    shards, rows, width = terms.shape
    half = rows // 2
    core = lax.axis_index("replica") % 2
    kept = lax.dynamic_slice(terms, (0, core * half, 0), (shards, half, width))
    sent = lax.dynamic_slice(terms, (0, (1 - core) * half, 0), (shards, half, width))
    both = (kept.astype(F32) + core_swap(sent).astype(F32)).astype(BF)
    return both


def finish(part):
    half, width = part.shape
    low = part.astype(BF)
    total = low.astype(F32) + side_swap(low).astype(F32)
    other = core_swap(total)
    core = lax.axis_index("replica") % 2
    first = jnp.where(core == 0, total, other)
    second = jnp.where(core == 0, other, total)
    return jnp.concatenate([first, second], 0)


def small_block(parts, width):
    flat = jnp.concatenate(parts, -1)
    lead = flat.shape[:-1]
    pad = SMALL_ROWS * width - flat.shape[-1]
    flat = jnp.concatenate([flat, jnp.zeros(lead + (pad,), flat.dtype)], -1)
    return flat.reshape(lead + (SMALL_ROWS, width))


def columns(matrix, width):
    return [matrix[..., i * width : (i + 1) * width] for i in range(matrix.shape[-1] // width)]


def gelu_parts(u):
    rising = 0.5 * (1.0 + lax.erf(u * (1.0 / math.sqrt(2.0))))
    density = jnp.exp(-0.5 * u * u) * (1.0 / math.sqrt(2.0 * math.pi))
    return (u * rising).astype(BF), (rising + u * density).astype(BF)


def norm_parts(r):
    center = r - jnp.mean(r, -1, keepdims=True)
    spread_ = jnp.mean(center * center, -1, keepdims=True)
    scale = lax.rsqrt(spread_ + EPSILON)
    return center * scale, scale


def norm_back(dout, unit, scale, gain):
    e = dout * gain
    dr = (e - jnp.mean(e, -1, keepdims=True) - unit * jnp.mean(e * unit, -1, keepdims=True)) * scale
    return dr, jnp.sum(dout * unit, 0), jnp.sum(dout, 0)


def shards_body(
    tokens, cotangent, seq_units, seq_order, share_start,
    stacked_weight, query_bias, value_bias, out_weight, out_bias, first_gain, first_shift,
    up_weight, up_bias, down_weight, down_bias, second_gain, second_shift,
):
    row_count, width = tokens.shape
    dest_count = lax.axis_size("shard")
    replicas = lax.axis_size("replica")
    per_dest = row_count // dest_count
    my_index = lax.axis_index("shard")
    replica = lax.axis_index("replica")
    wrows = stacked_weight.shape[0]
    frows = down_weight.shape[0]

    source_rows, segments, landing = routing(
        seq_units[0], seq_order[0], share_start[0], row_count, dest_count
    )
    flat_rows = source_rows.reshape(-1)

    smalls = [query_bias, value_bias, out_bias, first_gain, first_shift, down_bias, second_gain, second_shift, up_bias]
    small = small_block(smalls, width)
    first_pack = jnp.concatenate(columns(stacked_weight, width) + [out_weight, small], 0)
    token_send = pick_rows(tokens, flat_rows)
    hidden = lax.all_to_all(
        token_send.reshape(dest_count, per_dest, width), "shard", split_axis=0, concat_axis=0, tiled=True
    ).reshape(row_count, width)
    gathered = spread(first_pack)
    part = lambda i: gathered[:, i * wrows : (i + 1) * wrows].reshape(dest_count * wrows, width)
    w_query, w_key, w_value, w_out = part(0), part(1), part(2), part(3)
    small_all = gathered[:, 4 * wrows :].reshape(dest_count, SMALL_ROWS * width)
    offsets = [wrows * i for i in range(9)]
    vec = lambda i, n=wrows: small_all[:, offsets[i] : offsets[i] + n].reshape(-1).astype(F32)
    query_add, value_add, out_add, gain_first, shift_first, down_add, gain_second, shift_second = [vec(i) for i in range(8)]
    up_add = vec(8, frows)

    quarter, fquarter = wrows // replicas, frows // replicas
    up_mine = lax.dynamic_slice(up_weight, (replica * quarter, 0), (quarter, up_weight.shape[1]))
    down_mine = lax.dynamic_slice(down_weight, (replica * fquarter, 0), (fquarter, width))
    second_pack = jnp.concatenate(columns(up_mine, width) + [down_mine], 0)
    second = lax.all_gather(second_pack, ("shard", "replica"), axis=0, tiled=False)
    ups = up_weight.shape[1] // width
    up_full = jnp.concatenate(
        [second[:, i * quarter : (i + 1) * quarter].reshape(dest_count * wrows, width) for i in range(ups)], 1
    )
    down_full = second[:, ups * quarter :].reshape(dest_count * frows, width)

    grad_send = pick_rows(cotangent, flat_rows)
    upstream = lax.all_to_all(
        grad_send.reshape(dest_count, per_dest, width), "shard", split_axis=0, concat_axis=0, tiled=True
    ).reshape(row_count, width).astype(F32)

    my_segments = lax.dynamic_index_in_dim(segments, my_index, 0, keepdims=False)
    seg_rows = jnp.tile(my_segments, dest_count)
    kinds = jnp.arange(LANES, dtype=jnp.int32)[None, :]
    augq = jnp.where(jnp.logical_and(seg_rows[:, None] == kinds, kinds < 3), 1.0, 0.0).astype(BF)
    augk = jnp.where(
        kinds < 3, jnp.where(seg_rows[:, None] == kinds, 0.0, PENALTY), jnp.where(kinds < 9, -1.0, 0.0)
    ).astype(BF)

    zero_add = jnp.zeros((width,), F32)
    w_stack = jnp.concatenate([w_query, w_key, w_value], 1)
    qkv = (dot(hidden, w_stack) + jnp.concatenate([query_add, zero_add, value_add])).astype(BF)
    mixed, aug = attend(qkv, augq, augk)
    unit1, scale1 = norm_parts(hidden.astype(F32) + dot(mixed, w_out) + out_add)
    normed = unit1 * gain_first + shift_first
    normed_low = normed.astype(BF)
    act, slope = gelu_parts(dot(normed_low, up_full) + up_add)
    unit2, scale2 = norm_parts(normed + dot(act, down_full) + down_add)
    result = (unit2 * gain_second + shift_second).astype(BF)

    d_r2, g_gain2, g_shift2 = norm_back(upstream, unit2, scale2, gain_second)
    d_z = d_r2.astype(BF)
    g_down = dot_tn(act, d_z)
    g_down_add = jnp.sum(d_z.astype(F32), 0)
    d_u = (dot_nt(d_z, down_full) * slope.astype(F32)).astype(BF)
    g_up = dot_tn(normed_low, d_u)
    g_up_add = jnp.sum(d_u.astype(F32), 0)
    d_r1, g_gain1, g_shift1 = norm_back(d_r2 + dot_nt(d_u, up_full), unit1, scale1, gain_first)
    d_o = d_r1.astype(BF)
    g_out = dot_tn(mixed, d_o)
    g_out_add = jnp.sum(d_o.astype(F32), 0)
    d_a = dot_nt(d_o, w_out).astype(BF)

    out_recv = lax.all_to_all(
        result.reshape(dest_count, per_dest, width), "shard", split_axis=0, concat_axis=0, tiled=True
    ).reshape(row_count, width)

    by_shard = lambda g: g.astype(BF).reshape(dest_count, -1, width)
    flat_small = lambda gs: small_block([g.astype(BF).reshape(dest_count, -1) for g in gs], width)
    first_terms = jnp.concatenate(
        [by_shard(g_down)]
        + [by_shard(c) for c in columns(g_up, width)]
        + [by_shard(g_out), flat_small([g_out_add, g_gain1, g_shift1, g_down_add, g_gain2, g_shift2, g_up_add])],
        1,
    )
    pair1 = share_sum(first_terms)
    sum1 = lax.psum_scatter(
        pair1.reshape(-1, width), "shard", scatter_dimension=0, tiled=True
    ).astype(F32)

    d_q, d_k, d_v = attend_back(qkv, aug, augk, mixed, d_a)
    g_q, g_k, g_v = dot_tn(hidden, d_q), dot_tn(hidden, d_k), dot_tn(hidden, d_v)
    g_q_add = jnp.sum(d_q.astype(F32), 0)
    g_v_add = jnp.sum(d_v.astype(F32), 0)
    d_x = (d_r1 + dot_nt(d_q, w_query) + dot_nt(d_k, w_key) + dot_nt(d_v, w_value)).astype(BF)
    input_recv = lax.all_to_all(
        d_x.reshape(dest_count, per_dest, width), "shard", split_axis=0, concat_axis=0, tiled=True
    ).reshape(row_count, width)

    second_terms = jnp.concatenate(
        [by_shard(g_q), by_shard(g_k), by_shard(g_v), flat_small([g_q_add, g_v_add])], 1
    )
    pair2 = share_sum(second_terms)
    got2 = lax.all_to_all(pair2, "shard", split_axis=0, concat_axis=0, tiled=True)
    sum2 = jnp.sum(got2.astype(F32), 0)

    final1 = finish(sum1)
    final2 = finish(sum2)

    layer_out = pick_rows(out_recv, landing)
    input_grad = pick_rows(input_recv, landing)

    up_parts = [final1[frows + i * wrows : frows + (i + 1) * wrows] for i in range(ups)]
    base = frows + ups * wrows
    tail1 = final1[base + wrows :].reshape(-1)
    tail2 = final2[3 * wrows :].reshape(-1)
    s1 = lambda i, n=wrows: tail1[i * wrows : i * wrows + n]
    return (
        layer_out,
        input_grad,
        jnp.concatenate([final2[i * wrows : (i + 1) * wrows] for i in range(3)], 1),
        tail2[:wrows],
        tail2[wrows : 2 * wrows],
        final1[base : base + wrows],
        s1(0),
        s1(1),
        s1(2),
        jnp.concatenate(up_parts, 1),
        s1(6, frows),
        final1[:frows],
        s1(3),
        s1(4),
        s1(5),
    )


def solution(mesh):
    rows = P(("replica", "shard"), None)
    table = P("replica", None)
    matrix = P("shard", None)
    vector = P("shard")
    weights = (
        matrix, vector, vector, matrix, vector, vector, vector,
        matrix, vector, matrix, vector, vector, vector,
    )
    return jax.shard_map(
        shards_body,
        mesh=mesh,
        in_specs=(rows, rows, table, table, table) + weights,
        out_specs=(rows, rows) + weights,
        check_vma=False,
    )
```

time: 944 us -> 540 us (0.57)
  matrix products: 250 us -> 98.7 us
  waiting for transfers between devices: 326 us -> 175 us
  blocking collectives: 129 us -> 0 us
  Pallas kernels: 0 us -> 81.9 us
  other arithmetic: 83.6 us -> 42.3 us
  local copies, waits for them, and re-layouts: 101 us -> 81 us
  starting transfers between devices: 28.6 us -> 40 us
    reduce_scatter x4 -> x1, waiting for transfers between devices: 199 us -> 21 us  [shards_body(): lax.psum_scatter(pair1.reshape(-1, width), 'shard', scatter_dimension=0,...]
    dot_general x54 -> x16, matrix products: 250 us -> 98.7 us  [the longest x6 35.1 us: dot_nt(): lax.dot_general(a, b, (((1,), (1,)), ((), ())), preferred_element_type=F32)]
    unnamed x2 -> x0, blocking collectives: 99.9 us -> none
    ppermute x0 -> x11, waiting for transfers between devices: none -> 97.1 us  [the longest x1 41.4 us: spread(): got = lax.ppermute(line, 'shard', [(s, s ^ 1) for s in range(shards)])]
    pallas_call x0 -> x6, Pallas kernels: none -> 81.9 us  [the longest x1 39.2 us: attend_back(): pl.pallas_call(attend_back_kernel, grid=(pairs,), in_specs=[mine, pl.Bloc...]
    all_gather x4 -> x1, waiting for transfers between devices: 61 us -> 0.02 us  [shards_body(): lax.all_gather(second_pack, ('shard', 'replica'), axis=0, tiled=False)]
    convert_element_type x29 -> x6, other arithmetic: 38.3 us -> 13.7 us  [the longest x2 11.8 us: share_sum(): both = (kept.astype(F32) + core_swap(sent).astype(F32)).astype(BF)]
    all_gather x1 -> x0, blocking collectives: 22.7 us -> none  [shards(): lax.all_gather(up_bias, 'shard', axis=0, tiled=True)]
  transfers between devices with their start and end apart: 13 -> 18, of which waited for: 6 -> 8; matrix products, arithmetic and copies ran while one was open for 40% -> 20% of each run, Pallas kernels for 0% -> 15%
where the time goes in v1:
time: 540 us; the launch traced here: 534 us
  waiting for transfers between devices  175 us (32%)
  matrix products  98.7 us (18%)
  Pallas kernels  81.9 us (15%)
  local copies, waits for them, and re-layouts  81 us (15%)
  other arithmetic  42.3 us (8%)
  starting transfers between devices  40 us (7%)
  between operations  15.2 us (3%)
    ppermute x1, waiting for transfers between devices, spread(): got = lax.ppermute(line, 'shard', [(s, s ^ 1) for s in range(shards)])  41.4 us
    pallas_call x1, Pallas kernels, attend_back(): pl.pallas_call(attend_back_kernel, grid=(pairs,), in_specs=[mine, pl.Bloc...  39.2 us
    all_to_all x1, waiting for transfers between devices, shards_body(): lax.all_to_all(pair2, 'shard', split_axis=0, concat_axis=0, tiled=True)  38.9 us
    ppermute x3, waiting for transfers between devices, spread(): got = lax.ppermute(own, 'shard', [(s, s ^ 2 * k) for s in range(shards)])  38.1 us
    dot_general x6, matrix products, dot_nt(): lax.dot_general(a, b, (((1,), (1,)), ((), ())), preferred_element_type=F32)  35.1 us
    dot_general x4, matrix products, dot(): return jnp.dot(a, b, preferred_element_type=F32)  32.5 us
    dot_general x6, matrix products, dot_tn(): lax.dot_general(a, b, (((0,), (0,)), ((), ())), preferred_element_type=F32)  31.1 us
    unnamed x87, local copies, waits for them, and re-layouts  26.4 us
  transfers between devices with their start and end apart: 18, of which 8 were waited for; matrix products, arithmetic and copies ran while one was open for 20% of the time, Pallas kernels for 15%

profile of v1, /device:TPU:9, one launch (start us, length us, event | category | flops | bytes accessed | tf_op | source)
XLA Modules:
  0.0 533.7 jit_solution(13289182855780554595)
XLA Ops:
  12.1 6.1 %concatenate.46 = bf16[12288]{0:T(1024)(128)(2,1)S(1)} concatenate(bf16[96]{0:T(256)(128)(2,1)} %param.24, bf16[96]{0:T(256)(128)(2,1)} %param.25, bf16[96]{0:T(256)(128)(2,1)} %param.27, bf16[96]{0:T(256)(128)(2,1)} %param.28, bf16[96]{0:T(256)(128)(2,1)} %param.29, bf16[96]{0:T(256)(128)(2,1)} %param.33, bf16[96]{0:T(256)(128)(2,1)} %param.34, bf16[96]{0:T(256)(128)(2,1)} %param.35, ...), dimensions={0} | concatenate | bytes 49152 | tf_op jit(solution)/shard_map/concatenate | solution.py:317
  29.7 13.6 %collective-permute-done = bf16[200,768]{1,0:T(8,128)(2,1)} collective-permute-done((bf16[200,768]{1,0:T(8,128)(2,1)}, bf16[200,768]{1,0:T(8,128)(2,1)}, u32[]{:S(2)}, u32[]{:S(2)}) %collective-permute-start) | collective-permute-done | bytes 307232 | tf_op jit(solution)/shard_map/ppermute | solution.py:281
  45.3 24.5 %collective-permute-done.2 = bf16[200,768]{1,0:T(8,128)(2,1)} collective-permute-done((bf16[200,768]{1,0:T(8,128)(2,1)}, bf16[200,768]{1,0:T(8,128)(2,1)}, u32[]{:S(2)}, u32[]{:S(2)}) %collective-permute-start.2) | collective-permute-done | bytes 307232 | tf_op jit(solution)/shard_map/ppermute | solution.py:281
  73.8 5.4 %pick_rows.6 = bf16[1024,768]{1,0:T(8,128)(2,1)} custom-call(s32[1024,1]{1,0:T(8,128)} %select_select_fusion.rows_ref, bf16[1024,768]{1,0:T(8,128)(2,1)} %values_ref.3), custom_call_target="tpu_custom_call" | custom-call | flops 1610612736 | bytes 3145728 | tf_op jit(solution)/shard_map/pick_rows/pallas_call | solution.py:72
  79.1 4.0 all-to-all-start.2
  85.9 41.4 %collective-permute-done.3 = bf16[4,200,768]{2,1,0:T(8,128)(2,1)} collective-permute-done((bf16[4,200,768]{2,1,0:T(8,128)(2,1)S(1)}, bf16[4,200,768]{2,1,0:T(8,128)(2,1)}, u32[]{:S(2)}, u32[]{:S(2)}) %collective-permute-start.3) | collective-permute-done | bytes 1228832 | tf_op jit(solution)/shard_map/ppermute | solution.py:283
  133.2 5.3 pick_rows.4
  138.5 5.1 all-to-all-start
  157.2 4.2 fusion.40
  161.4 17.5 %all-to-all-done = bf16[8,128,768]{2,1,0:T(8,128)(2,1)} async-done(((bf16[8,128,768]{2,1,0:T(8,128)(2,1)}), bf16[8,128,768]{2,1,0:T(8,128)(2,1)}, u32[]{:S(2)}, u32[]{:S(2)}) %all-to-all-start) | async-done | bytes 1572896 | tf_op jit(solution)/shard_map/all_to_all | solution.py:367
  178.9 8.1 %add_convert_fusion.1.q_ref.k_ref.v_ref = bf16[1024,2304]{1,0:T(8,128)(2,1)} fusion(bf16[1024,768]{1,0:T(8,128)(2,1)} %bitcast.11, f32[2304]{0:T(1024)S(1)} %pad_maximum_fusion.6, bf16[768,768]{1,0:T(8,128)(2,1)S(1)} %bitcast.123, bf16[768,768]{1,0:T(8,128)(2,1)} %bitcast.135, bf16[768,768]{1,0:T(8,128)(2,1)} %bitcast.133), kind=kOutput, calls=%fused_computation.10 | convolution fusion | flops 3639214080 | bytes 9839616 | tf_op jit(solution)/shard_map/dot_general | solution.py:23
  187.0 21.5 %attend.1 = (bf16[1024,768]{1,0:T(8,128)(2,1)}, bf16[1024,768]{1,0:T(8,128)(2,1)}) custom-call(bf16[1024,2304]{1,0:T(8,128)(2,1)} %add_convert_fusion.1.q_ref.k_ref.v_ref, bf16[1024,2304]{1,0:T(8,128)(2,1)} %add_convert_fusion.1.q_ref.k_ref.v_ref, bf16[1024,2304]{1,0:T(8,128)(2,1)} %add_convert_fusion.1.q_ref.k_ref.v_ref, ...), custom_call_target="tpu_custom_call" | custom-call | flops 12884901888 | bytes 7864320 | tf_op jit(solution)/shard_map/attend/pallas_call | solution.py:135
  222.0 13.2 %multiply_convert_fusion.1 = (bf16[1024,3072]{1,0:T(8,128)(2,1)}, f32[1024,3072]{1,0:T(8,128)}) fusion(f32[3072]{0:T(1024)S(1)} %reshape.507, bf16[768,768]{1,0:T(8,128)(2,1)S(1)} %bitcast.141, bf16[768,768]{1,0:T(8,128)(2,1)S(1)} %bitcast.143, bf16[768,768]{1,0:T(8,128)(2,1)} %bitcast.145, bf16[768,768]{1,0:T(8,128)(2,1)S(1)} %bitcast.139, ...), kind=kOutput, calls=%fused_computation.7 | convolution fusion | flops 4873519104 | bytes 26765312 | tf_op jit(solution)/shard_map/dot_general | solution.py:23
  235.2 7.4 %fusion.46 = (f32[1024]{0:T(1024)S(1)}, f32[1024,768]{1,0:T(8,128)S(1)}) fusion(f32[768]{0:T(1024)S(1)} %reshape.508, bf16[1024,3072]{1,0:T(8,128)(2,1)} %get-tuple-element.84, bf16[3072,768]{1,0:T(8,128)(2,1)S(1)} %bitcast.128, f32[768]{0:T(1024)S(1)} %reshape.506, f32[768]{0:T(1024)S(1)} %reshape.505, f32[1024]{0:T(1024)S(1)} %add_rsqrt_fusion.1, ...), kind=kOutput, calls=%fused_computation.165 | convolution fusion | flops 4837342208 | bytes 17323008 | tf_op jit(solution)/shard_map/dot_general | solution.py:23
  247.5 7.1 %convolution_convert_fusion.1 = bf16[3072,768]{1,0:T(8,128)(2,1)} fusion(bf16[1024,3072]{1,0:T(8,128)(2,1)S(1)} %bitcast.171, f32[1024,768]{1,0:T(8,128)S(1)} %get-tuple-element.39), kind=kOutput, calls=%fused_computation.12 | convolution fusion | flops 4834983936 | bytes 14155776 | tf_op jit(solution)/shard_map/dot_general | solution.py:31
  254.6 13.4 %fusion.47 = (bf16[3072]{0:T(1024)(128)(2,1)S(1)}, bf16[1024,3072]{1,0:T(8,128)(2,1)}) fusion(f32[1024,3072]{1,0:T(8,128)} %get-tuple-element.85, f32[3072]{0:T(1024)S(1)} %reshape.507, bf16[3072,768]{1,0:T(8,128)(2,1)S(1)} %bitcast.129, f32[1024,768]{1,0:T(8,128)S(1)} %get-tuple-element.39), kind=kOutput, calls=%fused_computation.166 | convolution fusion | flops 4876661760 | bytes 26757120 | tf_op jit(solution)/shard_map/dot_general | solution.py:27
  268.1 10.3 %multiply_reduce_fusion = (bf16[768]{0:T(1024)(128)(2,1)S(1)}, f32[1024]{0:T(1024)S(1)}, f32[1024]{0:T(1024)S(1)}, bf16[768]{0:T(1024)(128)(2,1)S(1)}, f32[1024,768]{1,0:T(8,128)}) fusion(f32[1024,768]{1,0:T(8,128)S(1)} %copy-done.2, f32[1024]{0:T(1024)S(1)} %add_rsqrt_fusion.1, f32[1024]{0:T(1024)S(1)} %broadcast_multiply_fusion.4, f32[768]{0:T(1024)S(1)} %reshape.505, ...), kind=kOutput, calls=%fused_computation.31 | convolution fusion | flops 4858572800 | bytes 20469760 | tf_op jit(solution)/shard_map/dot_general | solution.py:27
  278.4 10.0 %convolution_convert_fusion = bf16[768,3072]{1,0:T(8,128)(2,1)} fusion(bf16[1024,3072]{1,0:T(8,128)(2,1)} %get-tuple-element.90, f32[1024,768]{1,0:T(8,128)S(1)} %copy-done.2, f32[768]{0:T(1024)S(1)} %reshape.506, f32[768]{0:T(1024)S(1)} %reshape.505, f32[1024]{0:T(1024)S(1)} %add_rsqrt_fusion.1, f32[1024]{0:T(1024)S(1)} %broadcast_multiply_fusion.4), kind=kOutput, calls=%fused_computation.11 | convolution fusion | flops 4838129664 | bytes 14170112 | tf_op jit(solution)/shard_map/dot_general | solution.py:31
  308.1 5.2 constant_dynamic-slice_fusion
  313.8 6.5 %all-to-all-start.1 = ((bf16[8,128,768]{2,1,0:T(8,128)(2,1)}), bf16[8,128,768]{2,1,0:T(8,128)(2,1)}, u32[]{:S(2)}, u32[]{:S(2)}) async-start(bf16[8,128,768]{2,1,0:T(8,128)(2,1)} %bitcast.117), calls=%async_computation.1 | async-start | bytes 3145728 | tf_op jit(solution)/shard_map/all_to_all | solution.py:427
  324.2 7.9 %add_convert_fusion = bf16[8,440,768]{2,1,0:T(8,128)(2,1)} fusion(bf16[8,440,768]{2,1,0:T(8,128)(2,1)} %collective-permute-done.8, bf16[8,880,768]{2,1,0:T(8,128)(2,1)} %bitcast_dynamic-update-slice_fusion.8, s32[]{:T(128)S(6)} %select_n.203), kind=kLoop, calls=%fused_computation.9 | loop fusion | flops 10813440 | bytes 16220164 | tf_op jit(solution)/shard_map/convert_element_type | solution.py:298
  332.1 39.2 %attend_back.1 = (bf16[1024,768]{1,0:T(8,128)(2,1)}, bf16[1024,768]{1,0:T(8,128)(2,1)}, bf16[1024,768]{1,0:T(8,128)(2,1)}) custom-call(bf16[1024,2304]{1,0:T(8,128)(2,1)} %add_convert_fusion.1.q_ref.k_ref.v_ref, bf16[1024,2304]{1,0:T(8,128)(2,1)} %add_convert_fusion.1.q_ref.k_ref.v_ref, bf16[1024,2304]{1,0:T(8,128)(2,1)} %add_convert_fusion.1.q_ref.k_ref.v_ref, ...), custom_call_target="tpu_custom_call" | custom-call | flops 32212254720 | bytes 14155776 | tf_op jit(solution)/shard_map/attend_back/pallas_call | solution.py:225
  371.3 4.5 convolution_convert_fusion.5
  375.7 4.1 convolution_convert_fusion.6
  397.2 3.9 add_convert_fusion.2
  401.1 5.6 %all-to-all-start.4 = ((bf16[8,152,768]{2,1,0:T(8,128)(2,1)}), bf16[8,152,768]{2,1,0:T(8,128)(2,1)}, u32[]{:S(2)}, u32[]{:S(2)}) async-start(bf16[8,152,768]{2,1,0:T(8,128)(2,1)} %add_convert_fusion.2), calls=%async_computation.4 | async-start | bytes 3735552 | tf_op jit(solution)/shard_map/all_to_all | solution.py:457
  414.7 38.9 %all-to-all-done.4 = bf16[8,152,768]{2,1,0:T(8,128)(2,1)} async-done(((bf16[8,152,768]{2,1,0:T(8,128)(2,1)}), bf16[8,152,768]{2,1,0:T(8,128)(2,1)}, u32[]{:S(2)}, u32[]{:S(2)}) %all-to-all-start.4) | async-done | bytes 1867808 | tf_op jit(solution)/shard_map/all_to_all | solution.py:457
  453.6 6.7 %all-to-all-start.3 = ((bf16[8,128,768]{2,1,0:T(8,128)(2,1)}), bf16[8,128,768]{2,1,0:T(8,128)(2,1)S(1)}, u32[]{:S(2)}, u32[]{:S(2)}) async-start(bf16[8,128,768]{2,1,0:T(8,128)(2,1)} %bitcast.118), calls=%async_computation.3 | async-start | bytes 3145728 | tf_op jit(solution)/shard_map/all_to_all | solution.py:449
  463.4 21.0 %reduce-scatter.2.cloned.1.call-done = bf16[440,768]{1,0:T(8,128)(2,1)} async-done(((bf16[3520,768]{1,0:T(8,128)(2,1)}), bf16[440,768]{1,0:T(8,128)(2,1)}) %reduce-scatter.2.cloned.1.call-update) | async-done | bytes 675856 | tf_op jit(solution)/shard_map/reduce_scatter | solution.py:440
  487.3 13.7 %collective-permute-done.9 = bf16[440,768]{1,0:T(8,128)(2,1)S(1)} collective-permute-done((bf16[440,768]{1,0:T(8,128)(2,1)}, bf16[440,768]{1,0:T(8,128)(2,1)S(1)}, u32[]{:S(2)}, u32[]{:S(2)}) %collective-permute-start.9) | collective-permute-done | bytes 675872 | tf_op jit(solution)/shard_map/ppermute | solution.py:261
  505.8 5.3 pick_rows.5
  512.2 5.3 pick_rows.7
  (237 shorter events, 132.5 us)
Async XLA Ops:
  7.2 18.3 %copy-start.28 = (s32[1,16]{1,0:T(1,128)S(1)}, s32[1,16]{1,0:T(1,128)}, u32[]{:S(2)}) copy-start(s32[1,16]{1,0:T(1,128)} %param.20) | copy-start | bytes 196
  7.2 18.3 %copy-start.25 = (s32[1,16]{1,0:T(1,128)S(1)}, s32[1,16]{1,0:T(1,128)}, u32[]{:S(2)}) copy-start(s32[1,16]{1,0:T(1,128)} %param.21) | copy-start | bytes 196
  7.2 19.5 %copy-start.23 = (s32[1,16]{1,0:T(1,128)S(1)}, s32[1,16]{1,0:T(1,128)}, u32[]{:S(2)}) copy-start(s32[1,16]{1,0:T(1,128)} %param.22) | copy-start | bytes 196
  7.2 207.2 %all-gather.3.cloned.1.call-start = ((), (), s32[]{:S(2)}) async-start(), calls=%async_computation.7 | async-start | bytes 9732096 | tf_op jit(solution)/shard_map/all_gather | solution.py:383
  22.8 21.5 %collective-permute-start.1 = (bf16[200,768]{1,0:T(8,128)(2,1)}, bf16[200,768]{1,0:T(8,128)(2,1)}, u32[]{:S(2)}, u32[]{:S(2)}) collective-permute-start(bf16[200,768]{1,0:T(8,128)(2,1)} %get-tuple-element.43), channel_id=1, source_target_pairs={{0,4},{1,5},{2,6},{3,7},{4,0},{5,1},{6,2},{7,3},{8,12},{9,13},{10,... | collective-permute-start | bytes 921608 | tf_op jit(solution)/shard_map/ppermute | solution.py:281
  25.1 18.2 %collective-permute-start = (bf16[200,768]{1,0:T(8,128)(2,1)}, bf16[200,768]{1,0:T(8,128)(2,1)}, u32[]{:S(2)}, u32[]{:S(2)}) collective-permute-start(bf16[200,768]{1,0:T(8,128)(2,1)} %get-tuple-element.43), channel_id=1, source_target_pairs={{0,2},{1,3},{2,0},{3,1},{4,6},{5,7},{6,4},{7,5},{8,10},{9,11},{10,... | collective-permute-start | bytes 921608 | tf_op jit(solution)/shard_map/ppermute | solution.py:281
  25.3 44.5 %collective-permute-start.2 = (bf16[200,768]{1,0:T(8,128)(2,1)}, bf16[200,768]{1,0:T(8,128)(2,1)}, u32[]{:S(2)}, u32[]{:S(2)}) collective-permute-start(bf16[200,768]{1,0:T(8,128)(2,1)} %get-tuple-element.43), channel_id=1, source_target_pairs={{0,6},{1,7},{2,4},{3,5},{4,2},{5,3},{6,0},{7,1},{8,14},{9,15},{10,... | collective-permute-start | bytes 921608 | tf_op jit(solution)/shard_map/ppermute | solution.py:281
  70.8 56.5 %collective-permute-start.3 = (bf16[4,200,768]{2,1,0:T(8,128)(2,1)S(1)}, bf16[4,200,768]{2,1,0:T(8,128)(2,1)}, u32[]{:S(2)}, u32[]{:S(2)}) collective-permute-start(bf16[4,200,768]{2,1,0:T(8,128)(2,1)S(1)} %bitcast_dynamic-update-slice_fusion.4), channel_id=1, source_target_pairs={{0,1},{1,0},{2,3},{3,2},{4,5},{5,4},{6,7},{7,6},{8,9},{9,8},{10,11... | collective-permute-start | bytes 3686408 | tf_op jit(solution)/shard_map/ppermute | solution.py:283
  79.1 59.4 %all-to-all-start.2 = ((bf16[8,128,768]{2,1,0:T(8,128)(2,1)}), bf16[8,128,768]{2,1,0:T(8,128)(2,1)S(1)}, u32[]{:S(2)}, u32[]{:S(2)}) async-start(bf16[8,128,768]{2,1,0:T(8,128)(2,1)} %bitcast.130), calls=%async_computation.2 | async-start | bytes 3145728 | tf_op jit(solution)/shard_map/all_to_all | solution.py:391
  129.8 22.0 %collective-permute-start.4 = (bf16[4,2,200,768]{3,2,1,0:T(8,128)(2,1)}, bf16[4,2,200,768]{3,2,1,0:T(8,128)(2,1)}, u32[]{:S(2)}, u32[]{:S(2)}) collective-permute-start(bf16[4,2,200,768]{3,2,1,0:T(8,128)(2,1)} %bitcast_dynamic-update-slice_fusion.3), channel_id=1, source_target_pairs={{0,8},{8,0},{16,24},{24,16},{1,9},{9,1},{17,25},{25,17},{2,10},{10... | collective-permute-start | bytes 7372808 | tf_op jit(solution)/shard_map/ppermute | solution.py:256
  138.5 40.4 %all-to-all-start = ((bf16[8,128,768]{2,1,0:T(8,128)(2,1)}), bf16[8,128,768]{2,1,0:T(8,128)(2,1)}, u32[]{:S(2)}, u32[]{:S(2)}) async-start(bf16[8,128,768]{2,1,0:T(8,128)(2,1)} %bitcast.131), calls=%async_computation | async-start | bytes 3145728 | tf_op jit(solution)/shard_map/all_to_all | solution.py:367
  161.4 25.6 %copy-start.8 = (bf16[8,96,768]{2,1,0:T(8,128)(2,1)}, bf16[8,96,768]{2,1,0:T(8,128)(2,1)S(1)}, u32[]{:S(2)}) copy-start(bf16[8,96,768]{2,1,0:T(8,128)(2,1)S(1)} %get-tuple-element.49) | copy-start | bytes 3538948
  220.9 14.3 %copy-start.16 = (bf16[32,24,768]{2,1,0:T(8,128)(2,1)}, bf16[32,24,768]{2,1,0:T(8,128)(2,1)S(1)}, u32[]{:S(2)}) copy-start(bf16[32,24,768]{2,1,0:T(8,128)(2,1)S(1)} %get-tuple-element.45) | copy-start | bytes 3538948
  220.9 14.3 %copy-start.18 = (bf16[32,24,768]{2,1,0:T(8,128)(2,1)}, bf16[32,24,768]{2,1,0:T(8,128)(2,1)S(1)}, u32[]{:S(2)}) copy-start(bf16[32,24,768]{2,1,0:T(8,128)(2,1)S(1)} %get-tuple-element.46) | copy-start | bytes 3538948
  254.6 13.5 %copy-start.17 = (bf16[32,24,768]{2,1,0:T(8,128)(2,1)S(1)}, bf16[32,24,768]{2,1,0:T(8,128)(2,1)}, u32[]{:S(2)}) copy-start(bf16[32,24,768]{2,1,0:T(8,128)(2,1)} %copy-done.16) | copy-start | bytes 3538948
  254.6 13.5 %copy-start.19 = (bf16[32,24,768]{2,1,0:T(8,128)(2,1)S(1)}, bf16[32,24,768]{2,1,0:T(8,128)(2,1)}, u32[]{:S(2)}) copy-start(bf16[32,24,768]{2,1,0:T(8,128)(2,1)} %copy-done.18) | copy-start | bytes 3538948
  254.6 13.5 %copy-start.20 = (bf16[32,24,768]{2,1,0:T(8,128)(2,1)S(1)}, bf16[32,24,768]{2,1,0:T(8,128)(2,1)}, u32[]{:S(2)}) copy-start(bf16[32,24,768]{2,1,0:T(8,128)(2,1)} %get-tuple-element.47) | copy-start | bytes 3538948
  313.4 10.8 %collective-permute-start.8 = (bf16[8,440,768]{2,1,0:T(8,128)(2,1)}, bf16[8,440,768]{2,1,0:T(8,128)(2,1)}, u32[]{:S(2)}, u32[]{:S(2)}) collective-permute-start(bf16[8,440,768]{2,1,0:T(8,128)(2,1)} %constant_dynamic-slice_fusion), channel_id=1, source_target_pairs={{0,8},{8,0},{16,24},{24,16},{1,9},{9,1},{17,25},{25,17},{2,10},{10... | collective-permute-start | bytes 16220168 | tf_op jit(solution)/shard_map/ppermute | solution.py:256
  313.8 87.3 %all-to-all-start.1 = ((bf16[8,128,768]{2,1,0:T(8,128)(2,1)}), bf16[8,128,768]{2,1,0:T(8,128)(2,1)}, u32[]{:S(2)}, u32[]{:S(2)}) async-start(bf16[8,128,768]{2,1,0:T(8,128)(2,1)} %bitcast.117), calls=%async_computation.1 | async-start | bytes 3145728 | tf_op jit(solution)/shard_map/all_to_all | solution.py:427
  320.3 164.1 %reduce-scatter.2.cloned.1.call-start = ((), (), s32[]{:S(2)}) async-start(), calls=%async_computation.6 | async-start | bytes 6082560 | tf_op jit(solution)/shard_map/reduce_scatter | solution.py:440
  393.0 4.2 collective-permute-start.5
  401.1 52.5 %all-to-all-start.4 = ((bf16[8,152,768]{2,1,0:T(8,128)(2,1)}), bf16[8,152,768]{2,1,0:T(8,128)(2,1)}, u32[]{:S(2)}, u32[]{:S(2)}) async-start(bf16[8,152,768]{2,1,0:T(8,128)(2,1)} %add_convert_fusion.2), calls=%async_computation.4 | async-start | bytes 3735552 | tf_op jit(solution)/shard_map/all_to_all | solution.py:457
  414.7 45.7 %copy-start.24 = (s32[1,16]{1,0:T(1,128)S(1)}, s32[1,16]{1,0:T(1,128)}, u32[]{:S(2)}) copy-start(s32[1,16]{1,0:T(1,128)} %param.22) | copy-start | bytes 196
  414.7 45.7 %copy-start.29 = (s32[1,16]{1,0:T(1,128)S(1)}, s32[1,16]{1,0:T(1,128)}, u32[]{:S(2)}) copy-start(s32[1,16]{1,0:T(1,128)} %param.20) | copy-start | bytes 196
  414.7 71.0 %copy-start.26 = (s32[16]{0:T(128)S(1)}, s32[16]{0:T(128)}, u32[]{:S(2)}) copy-start(s32[16]{0:T(128)} %get-tuple-element.36) | copy-start | bytes 196
  414.7 71.0 %copy-start.27 = (s32[16]{0:T(128)S(1)}, s32[16]{0:T(128)}, u32[]{:S(2)}) copy-start(s32[16]{0:T(128)} %get-tuple-element.37) | copy-start | bytes 196
  453.6 57.5 %all-to-all-start.3 = ((bf16[8,128,768]{2,1,0:T(8,128)(2,1)}), bf16[8,128,768]{2,1,0:T(8,128)(2,1)S(1)}, u32[]{:S(2)}, u32[]{:S(2)}) async-start(bf16[8,128,768]{2,1,0:T(8,128)(2,1)} %bitcast.118), calls=%async_computation.3 | async-start | bytes 3145728 | tf_op jit(solution)/shard_map/all_to_all | solution.py:449
  462.1 23.7 %collective-permute-start.6 = (bf16[152,768]{1,0:T(8,128)(2,1)S(1)}, bf16[152,768]{1,0:T(8,128)(2,1)S(1)}, u32[]{:S(2)}, u32[]{:S(2)}) collective-permute-start(bf16[152,768]{1,0:T(8,128)(2,1)S(1)} %reduce_sum.243), channel_id=1, source_target_pairs={{0,16},{8,24},{16,0},{24,8},{1,17},{9,25},{17,1},{25,9},{2,18},{10... | collective-permute-start | bytes 700424 | tf_op jit(solution)/shard_map/ppermute | solution.py:261
  484.4 16.6 %collective-permute-start.9 = (bf16[440,768]{1,0:T(8,128)(2,1)}, bf16[440,768]{1,0:T(8,128)(2,1)S(1)}, u32[]{:S(2)}, u32[]{:S(2)}) collective-permute-start(bf16[440,768]{1,0:T(8,128)(2,1)} %reduce-scatter.2.cloned.1.call-done), channel_id=1, source_target_pairs={{0,16},{8,24},{16,0},{24,8},{1,17},{9,25},{17,1},{25,9},{2,18},{10... | collective-permute-start | bytes 2027528 | tf_op jit(solution)/shard_map/ppermute | solution.py:261
  485.8 25.2 %copy-start.21 = (bf16[152,768]{1,0:T(8,128)(2,1)}, bf16[152,768]{1,0:T(8,128)(2,1)S(1)}, u32[]{:S(2)}) copy-start(bf16[152,768]{1,0:T(8,128)(2,1)S(1)} %collective-permute-done.6) | copy-start | bytes 700420
  486.7 30.8 %collective-permute-start.7 = (f32[152,768]{1,0:T(8,128)}, f32[152,768]{1,0:T(8,128)}, u32[]{:S(2)}, u32[]{:S(2)}) collective-permute-start(f32[152,768]{1,0:T(8,128)} %convert_add_fusion.1), channel_id=1, source_target_pairs={{0,8},{8,0},{16,24},{24,16},{1,9},{9,1},{17,25},{25,17},{2,10},{10... | collective-permute-start | bytes 1400840 | tf_op jit(solution)/shard_map/ppermute | solution.py:256
  503.6 16.8 %collective-permute-start.10 = (f32[440,768]{1,0:T(8,128)}, f32[440,768]{1,0:T(8,128)}, u32[]{:S(2)}, u32[]{:S(2)}) collective-permute-start(f32[440,768]{1,0:T(8,128)} %convert_add_fusion), channel_id=1, source_target_pairs={{0,8},{8,0},{16,24},{24,16},{1,9},{9,1},{17,25},{25,17},{2,10},{10... | collective-permute-start | bytes 4055048 | tf_op jit(solution)/shard_map/ppermute | solution.py:256
  (21 other events, 71.4 us)
Sparse Core Ops, SparseCore 0:
  12.1 126.5 all-gather.2
  332.2 152.1 reduce-scatter.1
